TPU v7x, 128 devices: a whole 4x4x4 slice. The times are simulated.
128 devices in a mesh: pipe: 4 (over z), dp: 32 (over y, x, core).
Axes of the slice: x: 4, y: 4, z: 4, core: 2. Of those that a mesh axis runs over, the one named last changes fastest.
Arguments:
- acts: bfloat16 [4, 4096, 5120], P('pipe', 'dp'), may hold values from -6 to 6
- cotangent: bfloat16 [4096, 5120], P('dp'), may hold values from -0.59765625 to 0.59765625
- kv_grads: bfloat16 [4, 4096, 2048], P('pipe', 'dp'), may hold values from -6 to 6
- w_kv: bfloat16 [4, 5120, 2048], P('pipe'), may hold values from -0.0078125 to 0.0078125
- momentum: bfloat16 [4, 5120, 2048], P('pipe', 'dp'), may hold values from -0.119628906 to 0.119628906
Outputs:
- update: bfloat16 [4, 5120, 2048], P('pipe', 'dp')
- input_grads: bfloat16 [4, 4096, 5120], P('pipe', 'dp')
All inputs are finite; a program needn't handle non-finite values.
Results may differ from a plain program's by a relative error of at most 0.022.
Values may be sent and summed in bfloat16 or wider, within the bound.
A program may use at most 128 MiB of HBM per device.

v0:
```python
import functools
import math

import jax
import jax.numpy as jnp
from jax import lax
from jax.experimental import pallas as pl
from jax.experimental.pallas import tpu as pltpu
from jax.sharding import PartitionSpec as P

MESH = pl.DeviceIdType.MESH
F32 = jnp.float32
BF16 = jnp.bfloat16
HEAD = 128
ITERS = 5
TOK = 128
D = 5120
COLS = 2048
HALF = 1024
ROWS = 320
OWN = 160
CH = 256
NCH = D // CH
ORDER = (2, 1, 3, 0)
FAR = (2, 1, 3)

momentum_rate = 0.95
quintic_a = 3.4445
quintic_b = -4.775
quintic_c = 2.0315
epsilon = 1e-07


def mod4(v):
    return lax.rem(v, 4)


def mm(a, b):
    return jnp.dot(a, b, preferred_element_type=F32, precision=lax.Precision.HIGHEST)


def newton_schulz(gram, scale):
    rows = lax.broadcasted_iota(jnp.int32, (HEAD, HEAD), 0)
    cols = lax.broadcasted_iota(jnp.int32, (HEAD, HEAD), 1)
    eye = (rows == cols).astype(F32)
    trace = jnp.sum(jnp.sum(gram * eye, axis=1, keepdims=True), axis=0, keepdims=True)
    inv = 1.0 / (jnp.sqrt(trace) + epsilon)
    a = (gram * inv) * inv
    q = None
    for step in range(ITERS):
        m = quintic_a * eye + quintic_b * a + quintic_c * mm(a, a)
        q = m if q is None else mm(q, m)
        if step < ITERS - 1:
            a = mm(mm(m, a), m)
    return q * (inv * scale)


def kernel(
    acts_h, cot_h, kv_h, w_h, mom_h, upd_o, ig_o,
    acts_v, acts_t, acts_g, kv_v, kv_g, w_v, part, acc, rbuf, mom_v, buf,
    gram, gram_r, tot, qall, upd, out_v, gin, gout,
    ld_sem, w_sem, kv_send, kv_recv, ac_send, ac_recv, rs_send, rs_recv,
    mom_send, mom_recv, ch_send, ch_recv, ig_sem, gr_send, gr_recv,
    t_send, t_recv, q_send, q_recv, o_send, o_recv, o_sem,
):
    z = lax.axis_index("pipe")
    d = lax.axis_index("dp")
    y, x, c = lax.div(d, 8), mod4(lax.div(d, 2)), lax.rem(d, 2)
    e = 1 - c
    pg = x * e + y * c
    pr = y * e + x * c

    def chip(yy, xx, cc):
        return (z, (mod4(yy) * 4 + mod4(xx)) * 2 + cc)

    def on_g(o):
        return chip(y + o * c, x + o * e, c)

    def on_r(o):
        return chip(y + o * e, x + o * c, c)

    sib = chip(y, x, e)
    bar = pltpu.get_barrier_semaphore()

    def greet(dev):
        pl.semaphore_signal(bar, inc=1, device_id=dev, device_id_type=MESH)

    for o in FAR:
        greet(on_g(o))
        greet(chip(y + o * c, x + o * e, e))
        greet(on_r(o))
    greet(sib)

    @pl.when(z < 3)
    def _():
        greet((z + 1, d))

    def start(cp):
        cp.start()
        return cp

    ld_kv = start(pltpu.make_async_copy(kv_h, kv_v, ld_sem.at[0]))
    ld_acts = start(pltpu.make_async_copy(acts_h, acts_v, ld_sem.at[1]))
    myrow = pl.multiple_of(c * OWN, OWN)
    mycol = pl.multiple_of(c * HALF, HALF)
    sibcol = pl.multiple_of(e * HALF, HALF)
    ld_mom = start(pltpu.make_async_copy(mom_h.at[:, pl.ds(mycol, HALF)], mom_v.at[pl.ds(myrow, OWN)], ld_sem.at[2]))

    @pl.loop(0, NCH)
    def _(k):
        pltpu.make_async_copy(w_h.at[pl.ds(pl.multiple_of(k * CH, CH), CH)], w_v.at[k], w_sem.at[k]).start()

    def cols(k):
        return pl.ds(pl.multiple_of(k * CH, CH), CH)

    @pl.when(z == 3)
    def _():
        @pl.loop(0, NCH)
        def _(k):
            pltpu.make_async_copy(cot_h.at[:, cols(k)], gin.at[:, cols(k)], ch_recv.at[k]).start()

    def remote(src, dst, ssem, rsem, dev):
        return pltpu.make_async_remote_copy(src, dst, ssem, rsem, device_id=dev, device_id_type=MESH)

    pl.semaphore_wait(bar, jnp.where(z > 0, 11, 10))

    sends = []
    ld_kv.wait()
    slots = (x * 2 + c, y * 2 + c)
    for i, off in enumerate(FAR):
        for t in (0, 1):
            dev = chip(y, x + off, 0) if t == 0 else chip(y + off, x, 1)
            sends.append(start(remote(
                kv_v.at[:, t * HALF:(t + 1) * HALF],
                kv_g.at[pl.ds(pl.multiple_of(slots[t] * TOK, TOK), TOK)],
                kv_send.at[i * 2 + t], kv_recv.at[slots[t]], dev)))
    slot_own = pg * 2 + c
    slot_sib = pr * 2 + c
    own_tok = pl.ds(pl.multiple_of(slot_own * TOK, TOK), TOK)
    sib_tok = pl.ds(pl.multiple_of(slot_sib * TOK, TOK), TOK)
    start(pltpu.make_async_copy(kv_v.at[:, pl.ds(mycol, HALF)], kv_g.at[own_tok], kv_recv.at[slot_own]))
    sends.append(start(remote(
        kv_v.at[:, pl.ds(sibcol, HALF)], kv_g.at[sib_tok], kv_send.at[6], kv_recv.at[slot_sib], sib)))
    sends.append(start(remote(
        mom_h.at[:, pl.ds(sibcol, HALF)], mom_v.at[pl.ds(myrow, OWN)], mom_send.at[0], mom_recv.at[0], sib)))

    ld_acts.wait()

    @pl.loop(0, D // 512)
    def _(k):
        at = pl.multiple_of(k * 512, 512)
        acts_t[pl.ds(at, 512), :] = acts_v[:, pl.ds(at, 512)].T

    n = 0
    for o in ORDER:
        for off in FAR:
            for t in (0, 1):
                if t == 0:
                    base = (mod4(y + o) * 4 + mod4(x + off)) * ROWS
                    dev = chip(y, x + off, 0)
                else:
                    base = (mod4(y + off) * 4 + mod4(x + o)) * ROWS
                    dev = chip(y + off, x, 1)
                sends.append(start(remote(
                    acts_t.at[pl.ds(pl.multiple_of(base, ROWS), ROWS)],
                    acts_g.at[o, :, pl.ds(pl.multiple_of(slots[t] * TOK, TOK), TOK)],
                    ac_send.at[n], ac_recv.at[o, slots[t]], dev)))
                n += 1
        base_own = (mod4(y + o * e) * 4 + mod4(x + o * c)) * ROWS
        base_sib = (mod4(y + o * c) * 4 + mod4(x + o * e)) * ROWS
        start(pltpu.make_async_copy(
            acts_t.at[pl.ds(pl.multiple_of(base_own, ROWS), ROWS)], acts_g.at[o, :, own_tok], ac_recv.at[o, slot_own]))
        sends.append(start(remote(
            acts_t.at[pl.ds(pl.multiple_of(base_sib, ROWS), ROWS)], acts_g.at[o, :, sib_tok],
            ac_send.at[n], ac_recv.at[o, slot_sib], sib)))
        n += 1

    def chain(lo, hi):
        @pl.loop(lo, hi)
        def _(k):
            pltpu.make_async_copy(w_h.at[pl.ds(0, CH)], w_v.at[k], w_sem.at[k]).wait()
            own = lax.dot_general(kv_v[...], w_v[k], (((1,), (1,)), ((), ())), preferred_element_type=F32)
            pltpu.make_async_copy(cot_h.at[:, cols(k)], gin.at[:, cols(k)], ch_recv.at[k]).wait()
            gout[:, cols(k)] = (gin[:, cols(k)].astype(F32) + own).astype(BF16)

            @pl.when(z > 0)
            def _():
                remote(gout.at[:, cols(k)], gin.at[:, cols(k)], ch_send.at[k], ch_recv.at[k], (z - 1, d)).start()

            pltpu.make_async_copy(gout.at[:, cols(k)], ig_o.at[:, cols(k)], ig_sem.at[k]).start()

    at = 0
    for i, o in enumerate(ORDER):
        upto = jnp.where(z == 3, NCH, (2, 4, 7, 9)[i] + 2 * z)
        chain(at, upto)
        at = upto
        if i == 0:
            for s in range(8):
                ref = kv_g.at[s * TOK:(s + 1) * TOK]
                pltpu.make_async_copy(ref, ref, kv_recv.at[s]).wait()
        for s in range(8):
            ref = acts_g.at[o, :, s * TOK:(s + 1) * TOK]
            pltpu.make_async_copy(ref, ref, ac_recv.at[o, s]).wait()

        @pl.loop(0, HALF // 256)
        def _(j):
            span = pl.ds(pl.multiple_of(j * 256, 256), 256)
            term = jnp.dot(acts_g[o], kv_g[:, span], preferred_element_type=F32)
            if o == 0:
                acc[:, span] = term
            else:
                part[o - 1, :, span] = term.astype(BF16)

        if o != 0:
            sends.append(start(remote(part.at[o - 1], rbuf.at[o - 1], rs_send.at[o - 1], rs_recv.at[o - 1], on_r(o))))
    chain(at, NCH)

    ld_mom.wait()
    half_mom = mom_v.at[pl.ds(pl.multiple_of(e * OWN, OWN), OWN)]
    pltpu.make_async_copy(half_mom, half_mom, mom_recv.at[0]).wait()
    for o in FAR:
        ref = rbuf.at[o - 1]
        pltpu.make_async_copy(ref, ref, rs_recv.at[o - 1]).wait()

    for h in range(8):
        span = slice(h * HEAD, (h + 1) * HEAD)
        grad = acc[:, span] + rbuf[0, :, span].astype(F32) + rbuf[1, :, span].astype(F32) + rbuf[2, :, span].astype(F32)
        value = (momentum_rate * mom_v[:, span].astype(F32) + grad * (1.0 / 4096)).astype(BF16)
        buf[:, span] = value
        gram[h // 2, h % 2] = lax.dot_general(value, value, (((0,), (0,)), ((), ())), preferred_element_type=F32)

    for o in FAR:
        sends.append(start(remote(gram.at[mod4(pg + o)], gram_r.at[o - 1], gr_send.at[o - 1], gr_recv.at[o - 1], on_g(o))))
    for o in FAR:
        ref = gram_r.at[o - 1]
        pltpu.make_async_copy(ref, ref, gr_recv.at[o - 1]).wait()
    tot[pr] = gram[pg] + gram_r[0] + gram_r[1] + gram_r[2]
    for o in FAR:
        sends.append(start(remote(tot.at[pr], tot.at[pr], t_send.at[o - 1], t_recv.at[o - 1], on_r(o))))
    for o in FAR:
        ref = tot.at[mod4(pr + 4 - o)]
        pltpu.make_async_copy(ref, ref, t_recv.at[o - 1]).wait()
    scale = 0.2 * math.sqrt(max(D, HEAD))
    for h in range(2):
        qall[pg, h] = newton_schulz(tot[0, h] + tot[1, h] + tot[2, h] + tot[3, h], scale)
    for o in FAR:
        sends.append(start(remote(qall.at[pg], qall.at[pg], q_send.at[o - 1], q_recv.at[o - 1], on_g(o))))
    for o in FAR:
        ref = qall.at[mod4(pg + 4 - o)]
        pltpu.make_async_copy(ref, ref, q_recv.at[o - 1]).wait()

    for h in range(8):
        span = slice(h * HEAD, (h + 1) * HEAD)
        q = qall[h // 2, h % 2]
        high = q.astype(BF16)
        rest = q - high.astype(F32)
        mid = rest.astype(BF16)
        low = (rest - mid.astype(F32)).astype(BF16)
        value = buf[:, span]
        total = jnp.dot(value, high, preferred_element_type=F32)
        total = total + jnp.dot(value, mid, preferred_element_type=F32)
        total = total + jnp.dot(value, low, preferred_element_type=F32)
        upd[:, span] = total.astype(BF16)

    sibrow = pl.multiple_of(e * OWN, OWN)
    swap = start(remote(upd.at[pl.ds(sibrow, OWN)], out_v, o_send.at[0], o_recv.at[0], sib))
    mine = start(pltpu.make_async_copy(upd.at[pl.ds(myrow, OWN)], upd_o.at[:, pl.ds(mycol, HALF)], o_sem.at[0]))
    pltpu.make_async_copy(out_v, out_v, o_recv.at[0]).wait()
    other = start(pltpu.make_async_copy(out_v, upd_o.at[:, pl.ds(sibcol, HALF)], o_sem.at[1]))
    for cp in sends:
        cp.wait_send()
    swap.wait_send()

    @pl.loop(0, NCH)
    def _(k):
        pltpu.make_async_copy(gout.at[:, cols(k)], ig_o.at[:, cols(k)], ig_sem.at[k]).wait()

    @pl.when(z > 0)
    def _():
        @pl.loop(0, NCH)
        def _(k):
            remote(gout.at[:, cols(k)], gin.at[:, cols(k)], ch_send.at[k], ch_recv.at[k], (z - 1, d)).wait_send()

    mine.wait()
    other.wait()


def shards(acts, cotangent, kv_grads, w_kv, momentum):
    dma = pltpu.SemaphoreType.DMA
    vmem = pltpu.VMEM
    anyspec = pl.BlockSpec(memory_space=pl.ANY)
    update, grads = pl.pallas_call(
        kernel,
        out_shape=(jax.ShapeDtypeStruct((OWN, COLS), BF16), jax.ShapeDtypeStruct((TOK, D), BF16)),
        in_specs=[anyspec] * 5,
        out_specs=(anyspec, anyspec),
        scratch_shapes=[
            vmem((TOK, D), BF16), vmem((D, TOK), BF16), vmem((4, ROWS, 8 * TOK), BF16),
            vmem((TOK, COLS), BF16), vmem((8 * TOK, HALF), BF16), vmem((NCH, CH, COLS), BF16),
            vmem((3, ROWS, HALF), BF16), vmem((ROWS, HALF), F32), vmem((3, ROWS, HALF), BF16),
            vmem((ROWS, HALF), BF16), vmem((ROWS, HALF), BF16),
            vmem((4, 2, HEAD, HEAD), F32), vmem((3, 2, HEAD, HEAD), F32), vmem((4, 2, HEAD, HEAD), F32),
            vmem((4, 2, HEAD, HEAD), F32), vmem((ROWS, HALF), BF16), vmem((OWN, HALF), BF16),
            vmem((TOK, D), BF16), vmem((TOK, D), BF16),
            dma((3,)), dma((NCH,)), dma((7,)), dma((8,)), dma((28,)), dma((4, 8)), dma((3,)), dma((3,)),
            dma((1,)), dma((1,)), dma((NCH,)), dma((NCH,)), dma((NCH,)), dma((3,)), dma((3,)),
            dma((3,)), dma((3,)), dma((3,)), dma((3,)), dma((1,)), dma((1,)), dma((2,)),
        ],
        name="muon_back",
        compiler_params=pltpu.CompilerParams(
            collective_id=0, has_side_effects=True, vmem_limit_bytes=60 * 1024 * 1024
        ),
    )(acts[0], cotangent, kv_grads[0], w_kv[0], momentum[0])
    return update[None], grads[None]


def solution(mesh):
    in_specs = (
        P("pipe", "dp", None),
        P("dp", None),
        P("pipe", "dp", None),
        P("pipe", None, None),
        P("pipe", "dp", None),
    )
    out_specs = (P("pipe", "dp", None), P("pipe", "dp", None))
    return jax.shard_map(shards, mesh=mesh, in_specs=in_specs, out_specs=out_specs, check_vma=False)
```

profile of v0, /device:TPU:1, one launch (start us, length us, event | category | flops | bytes accessed | tf_op | source)
XLA Modules:
  0.0 87.2 jit_solution(4231744139117939165)
XLA Ops:
  0.6 83.4 %muon_back.1 = (bf16[160,2048]{1,0:T(8,128)(2,1)}, bf16[128,5120]{1,0:T(8,128)(2,1)}) custom-call(bf16[128,5120]{1,0:T(8,128)(2,1)} %bitcast.7, bf16[128,5120]{1,0:T(8,128)(2,1)} %cot_h.1, bf16[128,2048]{1,0:T(8,128)(2,1)} %bitcast.11, bf16[5120,2048]{1,0:T(8,128)(2,1)} %bitcast.6, bf16[160,2048]{1,0:T(8,128)(2,1)} %bitcast.9), custom_call_target="tpu_custom_call" | custom-call | tf_op jit(solution)/shard_map/muon_back/pallas_call | solution.py:292
  84.1 0.0 copy-start
  84.1 2.1 %copy.9 = bf16[1,160,2048]{2,1,0:T(8,128)(2,1)} copy(bf16[1,160,2048]{2,1,0:T(8,128)(2,1)} %bitcast.10) | data formatting | bytes 1310720
  86.2 0.0 copy-done
  86.2 1.1 %copy.10 = bf16[1,128,5120]{2,1,0:T(8,128)(2,1)} copy(bf16[1,128,5120]{2,1,0:T(8,128)(2,1)S(1)} %bitcast.8) | data formatting | bytes 2621440
Async XLA Ops:
  84.1 2.1 %copy-start = (bf16[128,5120]{1,0:T(8,128)(2,1)S(1)}, bf16[128,5120]{1,0:T(8,128)(2,1)}, u32[]{:S(2)}) copy-start(bf16[128,5120]{1,0:T(8,128)(2,1)} %get-tuple-element.5) | copy-start | bytes 3932164
where the time goes:
time: 87.4 us; the launch traced here: 87.2 us
  Pallas kernels  83.4 us (95%)
  local copies, waits for them, and re-layouts  3.15 us (4%)
    pallas_call x1, Pallas kernels, shards(): pl.pallas_call(kernel, out_shape=(jax.ShapeDtypeStruct((OWN, COLS), BF16)...  83.4 us
    unnamed x4, local copies, waits for them, and re-layouts  3.15 us

commit v1 on v0

v1 whole, which is shorter than its diff:
```python
import functools
import math

import jax
import jax.numpy as jnp
from jax import lax
from jax.experimental import pallas as pl
from jax.experimental.pallas import tpu as pltpu
from jax.sharding import PartitionSpec as P

MESH = pl.DeviceIdType.MESH
F32 = jnp.float32
BF16 = jnp.bfloat16
HEAD = 128
ITERS = 5
TOK = 128
D = 5120
COLS = 2048
HALF = 1024
QC = 512
ROWS = 320
OWN = 160
CH = 256
NCH = D // CH
FAR = (2, 1, 3)

momentum_rate = 0.95
quintic_a = 3.4445
quintic_b = -4.775
quintic_c = 2.0315
epsilon = 1e-07


def mod4(v):
    return lax.rem(v, 4)


def split(a):
    high = a.astype(BF16)
    rest = a - high.astype(F32)
    mid = rest.astype(BF16)
    return high, mid, (rest - mid.astype(F32)).astype(BF16)


def mm(sa, sb):
    a1, a2, a3 = sa
    b1, b2, b3 = sb
    right = jnp.concatenate([jnp.concatenate([b2, b3], 1), jnp.concatenate([b1, b2], 1)], 0)
    small = jnp.dot(jnp.concatenate([a1, a2], 1), right, preferred_element_type=F32)
    big = jnp.dot(jnp.concatenate([a1, a3], 1), jnp.concatenate([b1, b1], 0), preferred_element_type=F32)
    return big + (small[:, :HEAD] + small[:, HEAD:])


def newton_schulz(gram, scale):
    rows = lax.broadcasted_iota(jnp.int32, (HEAD, HEAD), 0)
    cols = lax.broadcasted_iota(jnp.int32, (HEAD, HEAD), 1)
    eye = (rows == cols).astype(F32)
    trace = jnp.sum(jnp.sum(gram * eye, axis=1, keepdims=True), axis=0, keepdims=True)
    inv = 1.0 / (jnp.sqrt(trace) + epsilon)
    a = (gram * inv) * inv
    q = None
    for step in range(ITERS):
        sa = split(a)
        m = quintic_a * eye + quintic_b * a + quintic_c * mm(sa, sa)
        sm = split(m)
        q = m if q is None else mm(split(q), sm)
        if step < ITERS - 1:
            a = mm(split(mm(sm, sa)), sm)
    return q * (inv * scale)


def kernel(
    acts_h, cot_h, kv_h, w_h, mom_h, upd_o, ig_o,
    acts_v, acts_t, acts_g, kv_v, kv_g, w_v, part, trans, acc, rbuf, mom_v, buf,
    gram, gram_r, tot, qall, upd, out_v, gin, gout,
    ld_sem, w_sem, send_sem, kv_recv, kvf_recv, ac_recv, tr_recv, rs_recv,
    mom_recv, ch_send, ch_recv, ig_sem, gr_recv, t_recv, q_recv, o_recv, o_sem,
):
    z = lax.axis_index("pipe")
    d = lax.axis_index("dp")
    y, x, c = lax.div(d, 8), mod4(lax.div(d, 2)), lax.rem(d, 2)
    e = 1 - c
    pg = x * e + y * c
    pr = y * e + x * c

    def chip(yy, xx, cc):
        return (z, (mod4(yy) * 4 + mod4(xx)) * 2 + cc)

    def on_g(o):
        return chip(y + o * c, x + o * e, c)

    def on_r(o):
        return chip(y + o * e, x + o * c, c)

    sib = chip(y, x, e)
    bar = pltpu.get_barrier_semaphore()

    def greet(dev):
        pl.semaphore_signal(bar, inc=1, device_id=dev, device_id_type=MESH)

    for o in FAR:
        greet(on_g(o))
        greet(chip(y + o * c, x + o * e, e))
        greet(on_r(o))
    greet(sib)

    @pl.when(z < 3)
    def _():
        greet((z + 1, d))

    def start(cp):
        cp.start()
        return cp

    def remote(src, dst, ssem, rsem, dev):
        return pltpu.make_async_remote_copy(src, dst, ssem, rsem, device_id=dev, device_id_type=MESH)

    sends = []

    def send(src, dst, rsem, dev):
        sends.append(start(remote(src, dst, send_sem.at[len(sends)], rsem, dev)))

    def wait(ref, sem):
        pltpu.make_async_copy(ref, ref, sem).wait()

    def cols(k):
        return pl.ds(pl.multiple_of(k * CH, CH), CH)

    ld_kv = start(pltpu.make_async_copy(kv_h, kv_v, ld_sem.at[0]))
    ld_acts = start(pltpu.make_async_copy(acts_h, acts_v, ld_sem.at[1]))
    myrow = pl.multiple_of(c * OWN, OWN)
    sibrow = pl.multiple_of(e * OWN, OWN)
    mycol = pl.multiple_of(c * HALF, HALF)
    sibcol = pl.multiple_of(e * HALF, HALF)
    ld_mom = start(pltpu.make_async_copy(mom_h.at[:, pl.ds(mycol, HALF)], mom_v.at[pl.ds(myrow, OWN)], ld_sem.at[2]))

    @pl.loop(0, NCH)
    def _(k):
        pltpu.make_async_copy(w_h.at[pl.ds(pl.multiple_of(k * CH, CH), CH)], w_v.at[k], w_sem.at[k]).start()

    @pl.when(z == 3)
    def _():
        @pl.loop(0, NCH)
        def _(k):
            pltpu.make_async_copy(cot_h.at[:, cols(k)], gin.at[:, cols(k)], ch_recv.at[k]).start()

    pl.semaphore_wait(bar, jnp.where(z > 0, 11, 10))

    def toks(slot, first=0, count=TOK):
        return pl.ds(pl.multiple_of(slot * TOK + first, count), count)

    slots = (x * 2 + c, y * 2 + c)
    slot_own = pg * 2 + c
    slot_sib = pr * 2 + c
    ld_kv.wait()
    for q in range(2):
        for off in (1, 3):
            for t in (0, 1):
                dev = chip(y, x + off, 0) if t == 0 else chip(y + off, x, 1)
                at = t * HALF + q * QC
                send(kv_v.at[:, at:at + QC], kv_g.at[q, toks(slots[t])], kv_recv.at[q, off, c], dev)
        own_at = pl.ds(pl.multiple_of(mycol + q * QC, QC), QC)
        sib_at = pl.ds(pl.multiple_of(sibcol + q * QC, QC), QC)
        start(pltpu.make_async_copy(kv_v.at[:, own_at], kv_g.at[q, toks(slot_own)], kv_recv.at[q, 0, c]))
        send(kv_v.at[:, sib_at], kv_g.at[q, toks(slot_sib)], kv_recv.at[q, 0, c], sib)

    def chain(lo, hi):
        @pl.loop(lo, hi)
        def _(k):
            wait(w_v.at[k], w_sem.at[k])
            own = lax.dot_general(kv_v[...], w_v[k], (((1,), (1,)), ((), ())), preferred_element_type=F32)
            wait(gin.at[:, cols(k)], ch_recv.at[k])
            gout[:, cols(k)] = (gin[:, cols(k)].astype(F32) + own).astype(BF16)

            @pl.when(z > 0)
            def _():
                remote(gout.at[:, cols(k)], gin.at[:, cols(k)], ch_send.at[k], ch_recv.at[k], (z - 1, d)).start()

            pltpu.make_async_copy(gout.at[:, cols(k)], ig_o.at[:, cols(k)], ig_sem.at[k]).start()

    def steps(base, last):
        return jnp.where(z == 3, last, jnp.maximum(base + 2 * z, 0))

    at0 = steps(-100, 6)
    chain(0, at0)

    send(mom_h.at[:, pl.ds(sibcol, HALF)], mom_v.at[pl.ds(myrow, OWN)], mom_recv.at[0], sib)
    ld_acts.wait()

    @pl.loop(0, D // 512)
    def _(k):
        at = pl.multiple_of(k * 512, 512)
        acts_t[pl.ds(at, 512), :] = acts_v[:, pl.ds(at, 512)].T

    def send_acts(o):
        for off in FAR:
            for t in (0, 1):
                if t == 0:
                    base = (mod4(y + o) * 4 + mod4(x + off)) * ROWS
                    dev = chip(y, x + off, 0)
                else:
                    base = (mod4(y + off) * 4 + mod4(x + o)) * ROWS
                    dev = chip(y + off, x, 1)
                send(acts_t.at[pl.ds(pl.multiple_of(base, ROWS), ROWS)],
                     acts_g.at[o, :, toks(slots[t])], ac_recv.at[o, off, c], dev)
        base_own = (mod4(y + o * e) * 4 + mod4(x + o * c)) * ROWS
        base_sib = (mod4(y + o * c) * 4 + mod4(x + o * e)) * ROWS
        start(pltpu.make_async_copy(
            acts_t.at[pl.ds(pl.multiple_of(base_own, ROWS), ROWS)], acts_g.at[o, :, toks(slot_own)], ac_recv.at[o, 0, c]))
        send(acts_t.at[pl.ds(pl.multiple_of(base_sib, ROWS), ROWS)],
             acts_g.at[o, :, toks(slot_sib)], ac_recv.at[o, 0, c], sib)

    send_acts(2)
    send_acts(1)
    at1 = steps(0, 12)
    chain(at0, at1)
    for q in range(2):
        for off in (1, 3, 0):
            for cc in (0, 1):
                wait(kv_g.at[q, toks(mod4(pg + 4 - off) * 2 + cc)], kv_recv.at[q, off, cc])
                if off:
                    piece = kv_g.at[q, toks(mod4(pg + 4 - off) * 2 + cc, 0 if off == 1 else 64, 64)]
                    send(piece, piece, kvf_recv.at[q, off // 2, cc], on_g(off))
    send_acts(3)
    send_acts(0)
    at2 = steps(6, NCH)
    chain(at1, at2)
    for q in range(2):
        for half in range(2):
            for cc in (0, 1):
                wait(kv_g.at[q, toks(mod4(pg + 2) * 2 + cc, half * 64, 64)], kvf_recv.at[q, half, cc])

    def wait_acts(o):
        for off in range(4):
            for cc in (0, 1):
                wait(acts_g.at[o, :, toks(mod4(pg + 4 - off) * 2 + cc)], ac_recv.at[o, off, cc])

    def block(o, q):
        @pl.loop(0, QC // 256)
        def _(j):
            span = pl.ds(pl.multiple_of(j * 256, 256), 256)
            term = jnp.dot(acts_g[o], kv_g[q, :, span], preferred_element_type=F32)
            if o == 0:
                acc[q, :, span] = term
            elif o == 2:
                part[q, o - 1, :, span] = term.astype(BF16)
            elif o == 1:
                part[q, o - 1, :OWN, span] = (term[:OWN] + trans[q, 0, :, span].astype(F32)).astype(BF16)
                part[q, o - 1, OWN:, span] = term[OWN:].astype(BF16)
            else:
                part[q, o - 1, :OWN, span] = term[:OWN].astype(BF16)
                part[q, o - 1, OWN:, span] = (term[OWN:] + trans[q, 1, :, span].astype(F32)).astype(BF16)

    wait_acts(2)
    for q in range(2):
        block(2, q)
        send(part.at[q, 1, :OWN], trans.at[q, 0], tr_recv.at[q, 0], on_r(1))
        send(part.at[q, 1, OWN:], trans.at[q, 1], tr_recv.at[q, 1], on_r(3))
    at3 = steps(10, NCH)
    chain(at2, at3)
    wait_acts(1)
    wait_acts(3)
    for q in range(2):
        for o in (1, 3):
            wait(trans.at[q, o // 2], tr_recv.at[q, o // 2])
            block(o, q)
            send(part.at[q, o - 1], rbuf.at[q, o // 2], rs_recv.at[q, o // 2], on_r(o))
    wait_acts(0)
    for q in range(2):
        block(0, q)
    at4 = steps(16, NCH)
    at4 = jnp.minimum(at4, NCH)
    chain(at3, at4)

    ld_mom.wait()
    wait(mom_v.at[pl.ds(sibrow, OWN)], mom_recv.at[0])

    def gram_of(q):
        for s in range(2):
            wait(rbuf.at[q, s], rs_recv.at[q, s])
        for h in range(4):
            span = slice(h * HEAD, (h + 1) * HEAD)
            grad = acc[q, :, span] + rbuf[q, 0, :, span].astype(F32) + rbuf[q, 1, :, span].astype(F32)
            mom = mom_v[:, q * QC + h * HEAD:q * QC + (h + 1) * HEAD].astype(F32)
            value = (momentum_rate * mom + grad * (1.0 / 4096)).astype(BF16)
            buf[q, :, span] = value
            gram[q, h] = lax.dot_general(value, value, (((0,), (0,)), ((), ())), preferred_element_type=F32)
        for o in FAR:
            send(gram.at[q, mod4(pg + o)], gram_r.at[q, o - 1], gr_recv.at[q, o - 1], on_g(o))

    def combine(q):
        for o in FAR:
            wait(gram_r.at[q, o - 1], gr_recv.at[q, o - 1])
        tot[q, pr] = gram[q, pg] + gram_r[q, 0] + gram_r[q, 1] + gram_r[q, 2]
        for o in FAR:
            send(tot.at[q, pr], tot.at[q, pr], t_recv.at[q, o - 1], on_r(o))

    def iterate(q):
        for o in FAR:
            wait(tot.at[q, mod4(pr + 4 - o)], t_recv.at[q, o - 1])
        scale = 0.2 * math.sqrt(max(D, HEAD))
        qall[q, pg] = newton_schulz((tot[q, 0] + tot[q, 1]) + (tot[q, 2] + tot[q, 3]), scale)
        for o in FAR:
            send(qall.at[q, pg], qall.at[q, pg], q_recv.at[q, o - 1], on_g(o))

    outs = []

    def finish(q):
        for o in FAR:
            wait(qall.at[q, mod4(pg + 4 - o)], q_recv.at[q, o - 1])
        for h in range(4):
            span = slice(h * HEAD, (h + 1) * HEAD)
            high, mid, low = split(qall[q, h])
            value = buf[q, :, span]
            total = jnp.dot(value, low, preferred_element_type=F32) + jnp.dot(value, mid, preferred_element_type=F32)
            upd[q, :, span] = (total + jnp.dot(value, high, preferred_element_type=F32)).astype(BF16)
        send(upd.at[q, pl.ds(sibrow, OWN)], out_v.at[q], o_recv.at[q], sib)
        place = pl.ds(pl.multiple_of(mycol + q * QC, QC), QC)
        outs.append(start(pltpu.make_async_copy(upd.at[q, pl.ds(myrow, OWN)], upd_o.at[:, place], o_sem.at[q])))

    gram_of(0)
    chain(at4, NCH)
    combine(0)
    gram_of(1)
    iterate(0)
    combine(1)
    finish(0)
    iterate(1)
    finish(1)
    for q in range(2):
        wait(out_v.at[q], o_recv.at[q])
        place = pl.ds(pl.multiple_of(sibcol + q * QC, QC), QC)
        outs.append(start(pltpu.make_async_copy(out_v.at[q], upd_o.at[:, place], o_sem.at[2 + q])))
    for cp in sends:
        cp.wait_send()

    @pl.loop(0, NCH)
    def _(k):
        wait(gout.at[:, cols(k)], ig_sem.at[k])

    @pl.when(z > 0)
    def _():
        @pl.loop(0, NCH)
        def _(k):
            remote(gout.at[:, cols(k)], gin.at[:, cols(k)], ch_send.at[k], ch_recv.at[k], (z - 1, d)).wait_send()

    for cp in outs:
        cp.wait()


def shards(acts, cotangent, kv_grads, w_kv, momentum):
    dma = pltpu.SemaphoreType.DMA
    vmem = pltpu.VMEM
    anyspec = pl.BlockSpec(memory_space=pl.ANY)
    update, grads = pl.pallas_call(
        kernel,
        out_shape=(jax.ShapeDtypeStruct((OWN, COLS), BF16), jax.ShapeDtypeStruct((TOK, D), BF16)),
        in_specs=[anyspec] * 5,
        out_specs=(anyspec, anyspec),
        scratch_shapes=[
            vmem((TOK, D), BF16), vmem((D, TOK), BF16), vmem((4, ROWS, 8 * TOK), BF16),
            vmem((TOK, COLS), BF16), vmem((2, 8 * TOK, QC), BF16), vmem((NCH, CH, COLS), BF16),
            vmem((2, 3, ROWS, QC), BF16), vmem((2, 2, OWN, QC), BF16), vmem((2, ROWS, QC), F32),
            vmem((2, 2, ROWS, QC), BF16), vmem((ROWS, HALF), BF16), vmem((2, ROWS, QC), BF16),
            vmem((2, 4, HEAD, HEAD), F32), vmem((2, 3, HEAD, HEAD), F32), vmem((2, 4, HEAD, HEAD), F32),
            vmem((2, 4, HEAD, HEAD), F32), vmem((2, ROWS, QC), BF16), vmem((2, OWN, QC), BF16),
            vmem((TOK, D), BF16), vmem((TOK, D), BF16),
            dma((3,)), dma((NCH,)), dma((92,)), dma((2, 4, 2)), dma((2, 2, 2)), dma((4, 4, 2)),
            dma((2, 2)), dma((2, 2)), dma((1,)), dma((NCH,)), dma((NCH,)), dma((NCH,)), dma((2, 3)),
            dma((2, 3)), dma((2, 3)), dma((2,)), dma((4,)),
        ],
        name="muon_back",
        compiler_params=pltpu.CompilerParams(
            collective_id=0, has_side_effects=True, vmem_limit_bytes=60 * 1024 * 1024
        ),
    )(acts[0], cotangent, kv_grads[0], w_kv[0], momentum[0])
    return update[None], grads[None]


def solution(mesh):
    in_specs = (
        P("pipe", "dp", None),
        P("dp", None),
        P("pipe", "dp", None),
        P("pipe", None, None),
        P("pipe", "dp", None),
    )
    out_specs = (P("pipe", "dp", None), P("pipe", "dp", None))
    return jax.shard_map(shards, mesh=mesh, in_specs=in_specs, out_specs=out_specs, check_vma=False)
```

time: 87.4 us -> 83.6 us (0.957)
  Pallas kernels: 83.4 us -> 79.7 us
    pallas_call x1, Pallas kernels: 83.4 us -> 79.7 us  [shards(): pl.pallas_call(kernel, out_shape=(jax.ShapeDtypeStruct((OWN, COLS), BF16)...]
where the time goes in v1:
time: 83.6 us; the launch traced here: 83.5 us
  Pallas kernels  79.7 us (95%)
  local copies, waits for them, and re-layouts  3.15 us (4%)
    pallas_call x1, Pallas kernels, shards(): pl.pallas_call(kernel, out_shape=(jax.ShapeDtypeStruct((OWN, COLS), BF16)...  79.7 us
    unnamed x4, local copies, waits for them, and re-layouts  3.15 us

profile of v1, /device:TPU:1, one launch (start us, length us, event | category | flops | bytes accessed | tf_op | source)
XLA Modules:
  0.0 83.5 jit_solution(18235241914297349922)
XLA Ops:
  0.6 79.7 %muon_back.1 = (bf16[160,2048]{1,0:T(8,128)(2,1)}, bf16[128,5120]{1,0:T(8,128)(2,1)}) custom-call(bf16[128,5120]{1,0:T(8,128)(2,1)} %bitcast.7, bf16[128,5120]{1,0:T(8,128)(2,1)} %cot_h.1, bf16[128,2048]{1,0:T(8,128)(2,1)} %bitcast.11, bf16[5120,2048]{1,0:T(8,128)(2,1)} %bitcast.6, bf16[160,2048]{1,0:T(8,128)(2,1)} %bitcast.9), custom_call_target="tpu_custom_call" | custom-call | tf_op jit(solution)/shard_map/muon_back/pallas_call | solution.py:355
  80.4 0.0 copy-start
  80.4 2.1 %copy.9 = bf16[1,160,2048]{2,1,0:T(8,128)(2,1)} copy(bf16[1,160,2048]{2,1,0:T(8,128)(2,1)} %bitcast.10) | data formatting | bytes 1310720
  82.5 0.0 copy-done
  82.5 1.1 %copy.10 = bf16[1,128,5120]{2,1,0:T(8,128)(2,1)} copy(bf16[1,128,5120]{2,1,0:T(8,128)(2,1)S(1)} %bitcast.8) | data formatting | bytes 2621440
Async XLA Ops:
  80.4 2.1 %copy-start = (bf16[128,5120]{1,0:T(8,128)(2,1)S(1)}, bf16[128,5120]{1,0:T(8,128)(2,1)}, u32[]{:S(2)}) copy-start(bf16[128,5120]{1,0:T(8,128)(2,1)} %get-tuple-element.5) | copy-start | bytes 3932164

commit v2 on v1

--- a/solution.py
+++ b/solution.py
@@ -23,6 +23,17 @@
 CH = 256
 NCH = D // CH
 FAR = (2, 1, 3)
+PLAN = (
+    ((0, 0, 0, 6), (0, 0, 0, 6)),
+    ((10, 10, 4, 12), (0, 0, 1, 12)),
+    ((20, 20, 14, 20), (1, 4, 7, 20)),
+    ((20, 20, 20, 20), (5, 8, 12, 20)),
+    ((20, 20, 20, 20), (9, 12, 15, 20)),
+    ((20, 20, 20, 20), (11, 14, 17, 20)),
+    ((20, 20, 20, 20), (15, 18, 20, 20)),
+    ((20, 20, 20, 20), (18, 20, 20, 20)),
+    ((20, 20, 20, 20), (20, 20, 20, 20)),
+)
 
 momentum_rate = 0.95
 quintic_a = 3.4445
@@ -72,7 +83,7 @@
 def kernel(
     acts_h, cot_h, kv_h, w_h, mom_h, upd_o, ig_o,
     acts_v, acts_t, acts_g, kv_v, kv_g, w_v, part, trans, acc, rbuf, mom_v, buf,
-    gram, gram_r, tot, qall, upd, out_v, gin, gout,
+    gram, gram_r, tot, qall, upd, out_v, gin, gout, own_v,
     ld_sem, w_sem, send_sem, kv_recv, kvf_recv, ac_recv, tr_recv, rs_recv,
     mom_recv, ch_send, ch_recv, ig_sem, gr_recv, t_recv, q_recv, o_recv, o_sem,
 ):
@@ -142,7 +153,7 @@
     def _():
         @pl.loop(0, NCH)
         def _(k):
-            pltpu.make_async_copy(cot_h.at[:, cols(k)], gin.at[:, cols(k)], ch_recv.at[k]).start()
+            pltpu.make_async_copy(cot_h.at[:, cols(k)], gin.at[k], ch_recv.at[k]).start()
 
     pl.semaphore_wait(bar, jnp.where(z > 0, 11, 10))
 
@@ -164,25 +175,38 @@
         start(pltpu.make_async_copy(kv_v.at[:, own_at], kv_g.at[q, toks(slot_own)], kv_recv.at[q, 0, c]))
         send(kv_v.at[:, sib_at], kv_g.at[q, toks(slot_sib)], kv_recv.at[q, 0, c], sib)
 
-    def chain(lo, hi):
-        @pl.loop(lo, hi)
-        def _(k):
-            wait(w_v.at[k], w_sem.at[k])
-            own = lax.dot_general(kv_v[...], w_v[k], (((1,), (1,)), ((), ())), preferred_element_type=F32)
-            wait(gin.at[:, cols(k)], ch_recv.at[k])
-            gout[:, cols(k)] = (gin[:, cols(k)].astype(F32) + own).astype(BF16)
-
-            @pl.when(z > 0)
+    def product(k):
+        wait(w_v.at[k], w_sem.at[k])
+        own_v[k] = lax.dot_general(kv_v[...], w_v[k], (((1,), (1,)), ((), ())), preferred_element_type=F32)
+
+    def relay(k):
+        wait(gin.at[k], ch_recv.at[k])
+        gout[k] = (gin[k].astype(F32) + own_v[k]).astype(BF16)
+
+        @pl.when(z > 0)
+        def _():
+            remote(gout.at[k], gin.at[k], ch_send.at[k], ch_recv.at[k], (z - 1, d)).start()
+
+        pltpu.make_async_copy(gout.at[k], ig_o.at[:, cols(k)], ig_sem.at[k]).start()
+
+    done = [0, 0]
+
+    def chain(ahead, upto):
+        ready, sent = (jnp.where(z == 0, a[0], jnp.where(z == 1, a[1], jnp.where(z == 2, a[2], a[3]))) for a in (ahead, upto))
+
+        @pl.loop(0, jnp.maximum(ready - done[0], sent - done[1]))
+        def _(n):
+            @pl.when(done[0] + n < ready)
             def _():
-                remote(gout.at[:, cols(k)], gin.at[:, cols(k)], ch_send.at[k], ch_recv.at[k], (z - 1, d)).start()
-
-            pltpu.make_async_copy(gout.at[:, cols(k)], ig_o.at[:, cols(k)], ig_sem.at[k]).start()
-
-    def steps(base, last):
-        return jnp.where(z == 3, last, jnp.maximum(base + 2 * z, 0))
-
-    at0 = steps(-100, 6)
-    chain(0, at0)
+                product(done[0] + n)
+
+            @pl.when(done[1] + n < sent)
+            def _():
+                relay(done[1] + n)
+
+        done[:] = [ready, sent]
+
+    chain(*PLAN[0])
 
     send(mom_h.at[:, pl.ds(sibcol, HALF)], mom_v.at[pl.ds(myrow, OWN)], mom_recv.at[0], sib)
     ld_acts.wait()
@@ -211,9 +235,7 @@
              acts_g.at[o, :, toks(slot_sib)], ac_recv.at[o, 0, c], sib)
 
     send_acts(2)
-    send_acts(1)
-    at1 = steps(0, 12)
-    chain(at0, at1)
+    chain(*PLAN[1])
     for q in range(2):
         for off in (1, 3, 0):
             for cc in (0, 1):
@@ -221,10 +243,9 @@
                 if off:
                     piece = kv_g.at[q, toks(mod4(pg + 4 - off) * 2 + cc, 0 if off == 1 else 64, 64)]
                     send(piece, piece, kvf_recv.at[q, off // 2, cc], on_g(off))
+    send_acts(1)
     send_acts(3)
-    send_acts(0)
-    at2 = steps(6, NCH)
-    chain(at1, at2)
+    chain(*PLAN[2])
     for q in range(2):
         for half in range(2):
             for cc in (0, 1):
@@ -256,8 +277,8 @@
         block(2, q)
         send(part.at[q, 1, :OWN], trans.at[q, 0], tr_recv.at[q, 0], on_r(1))
         send(part.at[q, 1, OWN:], trans.at[q, 1], tr_recv.at[q, 1], on_r(3))
-    at3 = steps(10, NCH)
-    chain(at2, at3)
+    send_acts(0)
+    chain(*PLAN[3])
     wait_acts(1)
     wait_acts(3)
     for q in range(2):
@@ -268,9 +289,7 @@
     wait_acts(0)
     for q in range(2):
         block(0, q)
-    at4 = steps(16, NCH)
-    at4 = jnp.minimum(at4, NCH)
-    chain(at3, at4)
+    chain(*PLAN[4])
 
     ld_mom.wait()
     wait(mom_v.at[pl.ds(sibrow, OWN)], mom_recv.at[0])
@@ -319,13 +338,16 @@
         outs.append(start(pltpu.make_async_copy(upd.at[q, pl.ds(myrow, OWN)], upd_o.at[:, place], o_sem.at[q])))
 
     gram_of(0)
-    chain(at4, NCH)
+    chain(*PLAN[5])
     combine(0)
     gram_of(1)
+    chain(*PLAN[6])
+    combine(1)
     iterate(0)
-    combine(1)
+    chain(*PLAN[7])
+    iterate(1)
+    chain(*PLAN[8])
     finish(0)
-    iterate(1)
     finish(1)
     for q in range(2):
         wait(out_v.at[q], o_recv.at[q])
@@ -336,13 +358,13 @@
 
     @pl.loop(0, NCH)
     def _(k):
-        wait(gout.at[:, cols(k)], ig_sem.at[k])
+        wait(gout.at[k], ig_sem.at[k])
 
     @pl.when(z > 0)
     def _():
         @pl.loop(0, NCH)
         def _(k):
-            remote(gout.at[:, cols(k)], gin.at[:, cols(k)], ch_send.at[k], ch_recv.at[k], (z - 1, d)).wait_send()
+            remote(gout.at[k], gin.at[k], ch_send.at[k], ch_recv.at[k], (z - 1, d)).wait_send()
 
     for cp in outs:
         cp.wait()
@@ -364,7 +386,7 @@
             vmem((2, 2, ROWS, QC), BF16), vmem((ROWS, HALF), BF16), vmem((2, ROWS, QC), BF16),
             vmem((2, 4, HEAD, HEAD), F32), vmem((2, 3, HEAD, HEAD), F32), vmem((2, 4, HEAD, HEAD), F32),
             vmem((2, 4, HEAD, HEAD), F32), vmem((2, ROWS, QC), BF16), vmem((2, OWN, QC), BF16),
-            vmem((TOK, D), BF16), vmem((TOK, D), BF16),
+            vmem((NCH, TOK, CH), BF16), vmem((NCH, TOK, CH), BF16), vmem((NCH, TOK, CH), F32),
             dma((3,)), dma((NCH,)), dma((92,)), dma((2, 4, 2)), dma((2, 2, 2)), dma((4, 4, 2)),
             dma((2, 2)), dma((2, 2)), dma((1,)), dma((NCH,)), dma((NCH,)), dma((NCH,)), dma((2, 3)),
             dma((2, 3)), dma((2, 3)), dma((2,)), dma((4,)),

time: 83.6 us -> 74.1 us (0.89)
  Pallas kernels: 79.7 us -> 70.2 us
    pallas_call x1, Pallas kernels: 79.7 us -> 70.2 us  [shards(): pl.pallas_call(kernel, out_shape=(jax.ShapeDtypeStruct((OWN, COLS), BF16)...]
where the time goes in v2:
time: 74.1 us; the launch traced here: 74 us
  Pallas kernels  70.2 us (95%)
  local copies, waits for them, and re-layouts  3.15 us (4%)
    pallas_call x1, Pallas kernels, shards(): pl.pallas_call(kernel, out_shape=(jax.ShapeDtypeStruct((OWN, COLS), BF16)...  70.2 us
    unnamed x4, local copies, waits for them, and re-layouts  3.15 us

profile of v2, /device:TPU:1, one launch (start us, length us, event | category | flops | bytes accessed | tf_op | source)
XLA Modules:
  0.0 74.0 jit_solution(1831773925803006433)
XLA Ops:
  0.6 70.2 %muon_back.1 = (bf16[160,2048]{1,0:T(8,128)(2,1)}, bf16[128,5120]{1,0:T(8,128)(2,1)}) custom-call(bf16[128,5120]{1,0:T(8,128)(2,1)} %bitcast.7, bf16[128,5120]{1,0:T(8,128)(2,1)} %cot_h.1, bf16[128,2048]{1,0:T(8,128)(2,1)} %bitcast.11, bf16[5120,2048]{1,0:T(8,128)(2,1)} %bitcast.6, bf16[160,2048]{1,0:T(8,128)(2,1)} %bitcast.9), custom_call_target="tpu_custom_call" | custom-call | tf_op jit(solution)/shard_map/muon_back/pallas_call | solution.py:377
  70.8 0.0 copy-start
  70.8 2.1 %copy.9 = bf16[1,160,2048]{2,1,0:T(8,128)(2,1)} copy(bf16[1,160,2048]{2,1,0:T(8,128)(2,1)} %bitcast.10) | data formatting | bytes 1310720
  72.9 0.0 copy-done
  72.9 1.1 %copy.10 = bf16[1,128,5120]{2,1,0:T(8,128)(2,1)} copy(bf16[1,128,5120]{2,1,0:T(8,128)(2,1)S(1)} %bitcast.8) | data formatting | bytes 2621440
Async XLA Ops:
  70.8 2.1 %copy-start = (bf16[128,5120]{1,0:T(8,128)(2,1)S(1)}, bf16[128,5120]{1,0:T(8,128)(2,1)}, u32[]{:S(2)}) copy-start(bf16[128,5120]{1,0:T(8,128)(2,1)} %get-tuple-element.5) | copy-start | bytes 3932164

commit v3 on v2

v3 whole, which is shorter than its diff:
```python
import functools
import math

import jax
import jax.numpy as jnp
from jax import lax
from jax.experimental import pallas as pl
from jax.experimental.pallas import tpu as pltpu
from jax.sharding import PartitionSpec as P

MESH = pl.DeviceIdType.MESH
F32 = jnp.float32
BF16 = jnp.bfloat16
HEAD = 128
ITERS = 5
TOK = 128
D = 5120
COLS = 2048
HALF = 1024
PAIR = 256
ROWS = 320
OWN = 160
CH = 256
NCH = D // CH
FAR = (2, 1, 3)
ORDER = (2, 1, 3, 0)
PLAN = (
    ((0, 0, 0, 2), (0, 0, 0, 2)),
    ((5, 5, 4, 8), (0, 0, 1, 8)),
    ((20, 20, 20, 20), (6, 8, 11, 20)),
    ((20, 20, 20, 20), (8, 10, 13, 20)),
    ((20, 20, 20, 20), (11, 14, 17, 20)),
    ((20, 20, 20, 20), (13, 16, 19, 20)),
    ((20, 20, 20, 20), (17, 19, 20, 20)),
    ((20, 20, 20, 20), (20, 20, 20, 20)),
)

momentum_rate = 0.95
quintic_a = 3.4445
quintic_b = -4.775
quintic_c = 2.0315
epsilon = 1e-07


def mod4(v):
    return lax.rem(v, 4)


def split(a):
    high = a.astype(BF16)
    rest = a - high.astype(F32)
    mid = rest.astype(BF16)
    return high, mid, (rest - mid.astype(F32)).astype(BF16)


def mm(sa, sb):
    a1, a2, a3 = sa
    b1, b2, b3 = sb
    right = jnp.concatenate([jnp.concatenate([b2, b3], 1), jnp.concatenate([b1, b2], 1)], 0)
    small = jnp.dot(jnp.concatenate([a1, a2], 1), right, preferred_element_type=F32)
    big = jnp.dot(jnp.concatenate([a1, a3], 1), jnp.concatenate([b1, b1], 0), preferred_element_type=F32)
    return big + (small[:, :HEAD] + small[:, HEAD:])


def newton_schulz(gram, scale):
    rows = lax.broadcasted_iota(jnp.int32, (HEAD, HEAD), 0)
    cols = lax.broadcasted_iota(jnp.int32, (HEAD, HEAD), 1)
    eye = (rows == cols).astype(F32)
    trace = jnp.sum(jnp.sum(gram * eye, axis=1, keepdims=True), axis=0, keepdims=True)
    inv = 1.0 / (jnp.sqrt(trace) + epsilon)
    a = (gram * inv) * inv
    q = None
    for step in range(ITERS):
        sa = split(a)
        m = quintic_a * eye + quintic_b * a + quintic_c * mm(sa, sa)
        sm = split(m)
        q = m if q is None else mm(split(q), sm)
        if step < ITERS - 1:
            a = mm(split(mm(sm, sa)), sm)
    return q * (inv * scale)


def kernel(
    acts_h, cot_h, kv_h, w_h, mom_h, upd_o, ig_o,
    acts_v, acts_t, acts_g, kv_v, kv_g, w_v, part, trans, acc, rbuf, mom_v, buf,
    tot, upd, gin, gout, own_v,
    ld_sem, w_sem, send_sem, kv_recv, kvf_recv, ac_recv, tr_recv, rs_recv,
    mom_recv, ch_send, ch_recv, ig_sem, t_recv, o_recv,
):
    z = lax.axis_index("pipe")
    d = lax.axis_index("dp")
    y, x, c = lax.div(d, 8), mod4(lax.div(d, 2)), lax.rem(d, 2)
    e = 1 - c
    pg = x * e + y * c
    pr = y * e + x * c

    def chip(yy, xx, cc):
        return (z, (mod4(yy) * 4 + mod4(xx)) * 2 + cc)

    def on_g(o):
        return chip(y + o * c, x + o * e, c)

    def on_r(o):
        return chip(y + o * e, x + o * c, c)

    sib = chip(y, x, e)
    bar = pltpu.get_barrier_semaphore()

    def greet(dev):
        pl.semaphore_signal(bar, inc=1, device_id=dev, device_id_type=MESH)

    for o in FAR:
        greet(on_g(o))
        greet(chip(y + o * c, x + o * e, e))
        greet(on_r(o))
    greet(sib)

    @pl.when(z < 3)
    def _():
        greet((z + 1, d))

    def start(cp):
        cp.start()
        return cp

    def remote(src, dst, ssem, rsem, dev):
        return pltpu.make_async_remote_copy(src, dst, ssem, rsem, device_id=dev, device_id_type=MESH)

    sends = []

    def send(src, dst, rsem, dev):
        sends.append(start(remote(src, dst, send_sem.at[len(sends)], rsem, dev)))

    def wait(ref, sem):
        pltpu.make_async_copy(ref, ref, sem).wait()

    def cols(k):
        return pl.ds(pl.multiple_of(k * CH, CH), CH)

    ld_kv = start(pltpu.make_async_copy(kv_h, kv_v, ld_sem.at[0]))
    ld_acts = start(pltpu.make_async_copy(acts_h, acts_v, ld_sem.at[1]))
    myrow = pl.multiple_of(c * OWN, OWN)
    sibrow = pl.multiple_of(e * OWN, OWN)
    mycol = pl.multiple_of(c * HALF, HALF)
    sibcol = pl.multiple_of(e * HALF, HALF)
    ld_mom = start(pltpu.make_async_copy(mom_h.at[:, pl.ds(mycol, HALF)], mom_v.at[pl.ds(myrow, OWN)], ld_sem.at[2]))

    @pl.loop(0, NCH)
    def _(k):
        pltpu.make_async_copy(w_h.at[pl.ds(pl.multiple_of(k * CH, CH), CH)], w_v.at[k], w_sem.at[k]).start()

    @pl.when(z == 3)
    def _():
        @pl.loop(0, NCH)
        def _(k):
            pltpu.make_async_copy(cot_h.at[:, cols(k)], gin.at[k], ch_recv.at[k]).start()

    pl.semaphore_wait(bar, jnp.where(z > 0, 11, 10))

    def toks(slot, first=0, count=TOK):
        return pl.ds(pl.multiple_of(slot * TOK + first, count), count)

    slots = (x * 2 + c, y * 2 + c)
    slot_own = pg * 2 + c
    slot_sib = pr * 2 + c

    def near(off, cc):
        return mod4(pg + 4 - off) * 2 + cc

    def send_kv(o):
        at = (mod4(y + o) * PAIR, mod4(x + o) * PAIR + HALF)
        for off in (1, 3):
            for t in (0, 1):
                dev = chip(y, x + off, 0) if t == 0 else chip(y + off, x, 1)
                send(kv_v.at[:, pl.ds(pl.multiple_of(at[t], PAIR), PAIR)],
                     kv_g.at[o, toks(slots[t])], kv_recv.at[o, off, c], dev)
        own_at = pl.multiple_of(mod4(pr + o) * PAIR + mycol, PAIR)
        sib_at = pl.multiple_of(mod4(pg + o) * PAIR + sibcol, PAIR)
        start(pltpu.make_async_copy(kv_v.at[:, pl.ds(own_at, PAIR)], kv_g.at[o, toks(slot_own)], kv_recv.at[o, 0, c]))
        send(kv_v.at[:, pl.ds(sib_at, PAIR)], kv_g.at[o, toks(slot_sib)], kv_recv.at[o, 0, c], sib)

    def pass_kv(o):
        for off in (1, 3, 0):
            for cc in (0, 1):
                wait(kv_g.at[o, toks(near(off, cc))], kv_recv.at[o, off, cc])
                if off:
                    piece = kv_g.at[o, toks(near(off, cc), 0 if off == 1 else 64, 64)]
                    send(piece, piece, kvf_recv.at[o, off // 2, cc], on_g(off))

    def wait_far(o):
        for half in range(2):
            for cc in (0, 1):
                wait(kv_g.at[o, toks(near(2, cc), half * 64, 64)], kvf_recv.at[o, half, cc])

    ld_kv.wait()
    for o in FAR:
        send_kv(o)

    def product(k):
        wait(w_v.at[k], w_sem.at[k])
        own_v[k] = lax.dot_general(kv_v[...], w_v[k], (((1,), (1,)), ((), ())), preferred_element_type=F32)

    def relay(k):
        wait(gin.at[k], ch_recv.at[k])
        gout[k] = (gin[k].astype(F32) + own_v[k]).astype(BF16)

        @pl.when(z > 0)
        def _():
            remote(gout.at[k], gin.at[k], ch_send.at[k], ch_recv.at[k], (z - 1, d)).start()

        pltpu.make_async_copy(gout.at[k], ig_o.at[:, cols(k)], ig_sem.at[k]).start()

    done = [0, 0]

    def chain(ahead, upto):
        ready, sent = (jnp.where(z == 0, a[0], jnp.where(z == 1, a[1], jnp.where(z == 2, a[2], a[3]))) for a in (ahead, upto))

        @pl.loop(0, jnp.maximum(ready - done[0], sent - done[1]))
        def _(n):
            @pl.when(done[0] + n < ready)
            def _():
                product(done[0] + n)

            @pl.when(done[1] + n < sent)
            def _():
                relay(done[1] + n)

        done[:] = [ready, sent]

    chain(*PLAN[0])

    send(mom_h.at[:, pl.ds(sibcol, HALF)], mom_v.at[pl.ds(myrow, OWN)], mom_recv.at[0], sib)
    ld_acts.wait()

    @pl.loop(0, D // 512)
    def _(k):
        at = pl.multiple_of(k * 512, 512)
        acts_t[pl.ds(at, 512), :] = acts_v[:, pl.ds(at, 512)].T

    def send_acts(b):
        rows = pl.ds(b * ROWS, ROWS)

        def source(block):
            return acts_t.at[pl.ds(pl.multiple_of(block * ROWS, ROWS), ROWS)]

        for off in FAR:
            for t in (0, 1):
                block, dev = (b * 4 + mod4(x + off), chip(y, x + off, 0)) if t == 0 else (mod4(y + off) * 4 + b, chip(y + off, x, 1))
                send(source(block), acts_g.at[rows, toks(slots[t])], ac_recv.at[b, off, c], dev)
        start(pltpu.make_async_copy(
            source((b * 4 + x) * e + (y * 4 + b) * c), acts_g.at[rows, toks(slot_own)], ac_recv.at[b, 0, c]))
        send(source((b * 4 + x) * c + (y * 4 + b) * e), acts_g.at[rows, toks(slot_sib)], ac_recv.at[b, 0, c], sib)

    def half_rows(half):
        return pl.ds(half * 2 * ROWS, 2 * ROWS)

    def block(o):
        at = pl.ds(pl.multiple_of(mod4(pr + o) * PAIR, PAIR), PAIR)
        mom = mom_v[:, at].astype(F32) * momentum_rate
        for b in range(4):
            rows = pl.ds(b * ROWS, ROWS)
            term = jnp.dot(acts_g[rows, :], kv_g[o], preferred_element_type=F32)
            term = term + mom * jnp.where(pr == b, 4096.0, 0.0)
            if o == 2:
                part[1, 0, rows, :] = term[:, :HEAD].astype(BF16)
                part[1, 1, rows, :] = term[:, HEAD:].astype(BF16)
            else:
                acc[o, rows, :] = term

    send_acts(0)
    chain(*PLAN[1])
    for o in FAR:
        pass_kv(o)
    for b in (1, 2, 3):
        send_acts(b)
    send_kv(0)
    chain(*PLAN[2])
    for o in FAR:
        wait_far(o)
    ld_mom.wait()
    wait(mom_v.at[pl.ds(sibrow, OWN)], mom_recv.at[0])
    for b in range(4):
        for off in range(4):
            for cc in (0, 1):
                wait(acts_g.at[pl.ds(b * ROWS, ROWS), toks(near(off, cc))], ac_recv.at[b, off, cc])
    block(2)
    for q in range(2):
        for half in range(2):
            send(part.at[1, q, half_rows(half)], trans.at[q, half], tr_recv.at[q, half], on_r(1 + 2 * half))
    pass_kv(0)
    block(1)
    block(3)
    chain(*PLAN[3])
    for q in range(2):
        head = slice(q * HEAD, (q + 1) * HEAD)
        for half in range(2):
            o = 1 + 2 * half
            wait(trans.at[q, half], tr_recv.at[q, half])
            mine, other = half_rows(half), half_rows(1 - half)
            part[o - 1, q, mine, :] = (acc[o, mine, head] + trans[q, half].astype(F32)).astype(BF16)
            part[o - 1, q, other, :] = acc[o, other, head].astype(BF16)
            send(part.at[o - 1, q], rbuf.at[q, half], rs_recv.at[q, half], on_r(o))
    wait_far(0)
    block(0)
    chain(*PLAN[4])

    def gram_of(q):
        head = slice(q * HEAD, (q + 1) * HEAD)
        for half in range(2):
            wait(rbuf.at[q, half], rs_recv.at[q, half])
        total = None
        for b in range(4):
            rows = pl.ds(b * ROWS, ROWS)
            grad = acc[0, rows, head] + rbuf[q, 0, rows, :].astype(F32) + rbuf[q, 1, rows, :].astype(F32)
            value = (grad * (1.0 / 4096)).astype(BF16)
            buf[q, rows, :] = value
            term = lax.dot_general(value, value, (((0,), (0,)), ((), ())), preferred_element_type=F32)
            total = term if total is None else total + term
        tot[q, pg] = total
        for o in FAR:
            send(tot.at[q, pg], tot.at[q, pg], t_recv.at[q, o - 1], on_g(o))

    def iterate(q):
        for o in FAR:
            wait(tot.at[q, mod4(pg + 4 - o)], t_recv.at[q, o - 1])
        scale = 0.2 * math.sqrt(max(D, HEAD))
        high, mid, low = split(newton_schulz((tot[q, 0] + tot[q, 1]) + (tot[q, 2] + tot[q, 3]), scale))
        place = pl.ds(pl.multiple_of(mycol + pr * PAIR + q * HEAD, HEAD), HEAD)
        for o in ORDER:
            first = pl.multiple_of(mod4(pr + o) * ROWS, ROWS)
            value = buf[q, pl.ds(first, ROWS), :]
            total = jnp.dot(value, low, preferred_element_type=F32) + jnp.dot(value, mid, preferred_element_type=F32)
            upd[q, pl.ds(first, ROWS), :] = (total + jnp.dot(value, high, preferred_element_type=F32)).astype(BF16)
            same = upd.at[q, pl.ds(pl.multiple_of(first + myrow, OWN), OWN)]
            cross = upd.at[q, pl.ds(pl.multiple_of(first + sibrow, OWN), OWN)]
            if o:
                send(same, upd_o.at[:, place], o_recv.at[q, 0, o], on_r(o))
                send(cross, upd_o.at[:, place], o_recv.at[q, 1, o], chip(y + o * e, x + o * c, e))
            else:
                start(pltpu.make_async_copy(same, upd_o.at[:, place], o_recv.at[q, 0, 0]))
                send(cross, upd_o.at[:, place], o_recv.at[q, 1, 0], sib)

    gram_of(0)
    chain(*PLAN[5])
    gram_of(1)
    iterate(0)
    chain(*PLAN[6])
    iterate(1)
    chain(*PLAN[7])
    for q in range(2):
        for o in range(4):
            at = pl.multiple_of(mycol + mod4(pr + 4 - o) * PAIR + q * HEAD, HEAD)
            wait(upd_o.at[:, pl.ds(at, HEAD)], o_recv.at[q, 0, o])
            at = pl.multiple_of(sibcol + mod4(pg + 4 - o) * PAIR + q * HEAD, HEAD)
            wait(upd_o.at[:, pl.ds(at, HEAD)], o_recv.at[q, 1, o])
    for cp in sends:
        cp.wait_send()

    @pl.loop(0, NCH)
    def _(k):
        wait(gout.at[k], ig_sem.at[k])

    @pl.when(z > 0)
    def _():
        @pl.loop(0, NCH)
        def _(k):
            remote(gout.at[k], gin.at[k], ch_send.at[k], ch_recv.at[k], (z - 1, d)).wait_send()


def shards(acts, cotangent, kv_grads, w_kv, momentum):
    dma = pltpu.SemaphoreType.DMA
    vmem = pltpu.VMEM
    anyspec = pl.BlockSpec(memory_space=pl.ANY)
    update, grads = pl.pallas_call(
        kernel,
        out_shape=(jax.ShapeDtypeStruct((OWN, COLS), BF16), jax.ShapeDtypeStruct((TOK, D), BF16)),
        in_specs=[anyspec] * 5,
        out_specs=(anyspec, anyspec),
        scratch_shapes=[
            vmem((TOK, D), BF16), vmem((D, TOK), BF16), vmem((4 * ROWS, 8 * TOK), BF16),
            vmem((TOK, COLS), BF16), vmem((4, 8 * TOK, PAIR), BF16), vmem((NCH, CH, COLS), BF16),
            vmem((3, 2, 4 * ROWS, HEAD), BF16), vmem((2, 2, 2 * ROWS, HEAD), BF16), vmem((4, 4 * ROWS, PAIR), F32),
            vmem((2, 2, 4 * ROWS, HEAD), BF16), vmem((ROWS, HALF), BF16), vmem((2, 4 * ROWS, HEAD), BF16),
            vmem((2, 4, HEAD, HEAD), F32), vmem((2, 4 * ROWS, HEAD), BF16),
            vmem((NCH, TOK, CH), BF16), vmem((NCH, TOK, CH), BF16), vmem((NCH, TOK, CH), F32),
            dma((3,)), dma((NCH,)), dma((96,)), dma((4, 4, 2)), dma((4, 2, 2)), dma((4, 4, 2)),
            dma((2, 2)), dma((2, 2)), dma((1,)), dma((NCH,)), dma((NCH,)), dma((NCH,)),
            dma((2, 3)), dma((2, 2, 4)),
        ],
        name="muon_back",
        compiler_params=pltpu.CompilerParams(
            collective_id=0, has_side_effects=True, vmem_limit_bytes=60 * 1024 * 1024
        ),
    )(acts[0], cotangent, kv_grads[0], w_kv[0], momentum[0])
    return update[None], grads[None]


def solution(mesh):
    in_specs = (
        P("pipe", "dp", None),
        P("dp", None),
        P("pipe", "dp", None),
        P("pipe", None, None),
        P("pipe", "dp", None),
    )
    out_specs = (P("pipe", "dp", None), P("pipe", "dp", None))
    return jax.shard_map(shards, mesh=mesh, in_specs=in_specs, out_specs=out_specs, check_vma=False)
```

time: 74.1 us -> 77.7 us (1.049)
  Pallas kernels: 70.2 us -> 73.8 us
    pallas_call x1, Pallas kernels: 70.2 us -> 73.8 us  [shards(): pl.pallas_call(kernel, out_shape=(jax.ShapeDtypeStruct((OWN, COLS), BF16)...]
where the time goes in v3:
time: 77.7 us; the launch traced here: 77.6 us
  Pallas kernels  73.8 us (95%)
  local copies, waits for them, and re-layouts  3.15 us (4%)
    pallas_call x1, Pallas kernels, shards(): pl.pallas_call(kernel, out_shape=(jax.ShapeDtypeStruct((OWN, COLS), BF16)...  73.8 us
    unnamed x4, local copies, waits for them, and re-layouts  3.15 us

profile of v3, /device:TPU:1, one launch (start us, length us, event | category | flops | bytes accessed | tf_op | source)
XLA Modules:
  0.0 77.6 jit_solution(3187138569481893910)
XLA Ops:
  0.6 73.8 %muon_back.1 = (bf16[160,2048]{1,0:T(8,128)(2,1)}, bf16[128,5120]{1,0:T(8,128)(2,1)}) custom-call(bf16[128,5120]{1,0:T(8,128)(2,1)} %bitcast.7, bf16[128,5120]{1,0:T(8,128)(2,1)} %cot_h.1, bf16[128,2048]{1,0:T(8,128)(2,1)} %bitcast.11, bf16[5120,2048]{1,0:T(8,128)(2,1)} %bitcast.6, bf16[160,2048]{1,0:T(8,128)(2,1)} %bitcast.9), custom_call_target="tpu_custom_call" | custom-call | tf_op jit(solution)/shard_map/muon_back/pallas_call | solution.py:374
  74.4 0.0 copy-start
  74.4 2.1 %copy.9 = bf16[1,160,2048]{2,1,0:T(8,128)(2,1)} copy(bf16[1,160,2048]{2,1,0:T(8,128)(2,1)} %bitcast.10) | data formatting | bytes 1310720
  76.5 0.0 copy-done
  76.5 1.1 %copy.10 = bf16[1,128,5120]{2,1,0:T(8,128)(2,1)} copy(bf16[1,128,5120]{2,1,0:T(8,128)(2,1)S(1)} %bitcast.8) | data formatting | bytes 2621440
Async XLA Ops:
  74.4 2.1 %copy-start = (bf16[128,5120]{1,0:T(8,128)(2,1)S(1)}, bf16[128,5120]{1,0:T(8,128)(2,1)}, u32[]{:S(2)}) copy-start(bf16[128,5120]{1,0:T(8,128)(2,1)} %get-tuple-element.5) | copy-start | bytes 3932164

commit v4 on v3

--- a/solution.py
+++ b/solution.py
@@ -26,12 +26,17 @@
 ORDER = (2, 1, 3, 0)
 PLAN = (
     ((0, 0, 0, 2), (0, 0, 0, 2)),
-    ((5, 5, 4, 8), (0, 0, 1, 8)),
-    ((20, 20, 20, 20), (6, 8, 11, 20)),
-    ((20, 20, 20, 20), (8, 10, 13, 20)),
-    ((20, 20, 20, 20), (11, 14, 17, 20)),
-    ((20, 20, 20, 20), (13, 16, 19, 20)),
-    ((20, 20, 20, 20), (17, 19, 20, 20)),
+    ((5, 5, 4, 6), (0, 0, 1, 5)),
+    ((13, 13, 12, 14), (0, 2, 6, 9)),
+    ((13, 13, 12, 14), (0, 2, 6, 9)),
+    ((17, 17, 16, 18), (0, 4, 8, 12)),
+    ((20, 20, 20, 20), (2, 6, 10, 14)),
+    ((20, 20, 20, 20), (4, 8, 13, 17)),
+    ((20, 20, 20, 20), (5, 10, 15, 19)),
+    ((20, 20, 20, 20), (8, 13, 18, 20)),
+    ((20, 20, 20, 20), (10, 15, 20, 20)),
+    ((20, 20, 20, 20), (13, 18, 20, 20)),
+    ((20, 20, 20, 20), (13, 19, 20, 20)),
     ((20, 20, 20, 20), (20, 20, 20, 20)),
 )
 
@@ -254,18 +259,16 @@
     def half_rows(half):
         return pl.ds(half * 2 * ROWS, 2 * ROWS)
 
-    def block(o):
+    def block(o, b):
         at = pl.ds(pl.multiple_of(mod4(pr + o) * PAIR, PAIR), PAIR)
-        mom = mom_v[:, at].astype(F32) * momentum_rate
-        for b in range(4):
-            rows = pl.ds(b * ROWS, ROWS)
-            term = jnp.dot(acts_g[rows, :], kv_g[o], preferred_element_type=F32)
-            term = term + mom * jnp.where(pr == b, 4096.0, 0.0)
-            if o == 2:
-                part[1, 0, rows, :] = term[:, :HEAD].astype(BF16)
-                part[1, 1, rows, :] = term[:, HEAD:].astype(BF16)
-            else:
-                acc[o, rows, :] = term
+        rows = pl.ds(b * ROWS, ROWS)
+        term = jnp.dot(acts_g[rows, :], kv_g[o], preferred_element_type=F32)
+        term = term + (mom_v[:, at].astype(F32) * momentum_rate) * jnp.where(pr == b, 4096.0, 0.0)
+        if o == 2:
+            part[1, 0, rows, :] = term[:, :HEAD].astype(BF16)
+            part[1, 1, rows, :] = term[:, HEAD:].astype(BF16)
+        else:
+            acc[o, rows, :] = term
 
     send_acts(0)
     chain(*PLAN[1])
@@ -280,17 +283,19 @@
     ld_mom.wait()
     wait(mom_v.at[pl.ds(sibrow, OWN)], mom_recv.at[0])
     for b in range(4):
+        chain(*PLAN[3 + b])
         for off in range(4):
             for cc in (0, 1):
                 wait(acts_g.at[pl.ds(b * ROWS, ROWS), toks(near(off, cc))], ac_recv.at[b, off, cc])
-    block(2)
-    for q in range(2):
-        for half in range(2):
-            send(part.at[1, q, half_rows(half)], trans.at[q, half], tr_recv.at[q, half], on_r(1 + 2 * half))
+        block(2, b)
+        if b % 2:
+            half = b // 2
+            for q in range(2):
+                send(part.at[1, q, half_rows(half)], trans.at[q, half], tr_recv.at[q, half], on_r(1 + 2 * half))
+        block(1, b)
+        block(3, b)
     pass_kv(0)
-    block(1)
-    block(3)
-    chain(*PLAN[3])
+    chain(*PLAN[7])
     for q in range(2):
         head = slice(q * HEAD, (q + 1) * HEAD)
         for half in range(2):
@@ -301,8 +306,9 @@
             part[o - 1, q, other, :] = acc[o, other, head].astype(BF16)
             send(part.at[o - 1, q], rbuf.at[q, half], rs_recv.at[q, half], on_r(o))
     wait_far(0)
-    block(0)
-    chain(*PLAN[4])
+    for b in range(4):
+        block(0, b)
+    chain(*PLAN[8])
 
     def gram_of(q):
         head = slice(q * HEAD, (q + 1) * HEAD)
@@ -341,12 +347,12 @@
                 send(cross, upd_o.at[:, place], o_recv.at[q, 1, 0], sib)
 
     gram_of(0)
-    chain(*PLAN[5])
+    chain(*PLAN[9])
     gram_of(1)
     iterate(0)
-    chain(*PLAN[6])
+    chain(*PLAN[10])
     iterate(1)
-    chain(*PLAN[7])
+    chain(*PLAN[12])
     for q in range(2):
         for o in range(4):
             at = pl.multiple_of(mycol + mod4(pr + 4 - o) * PAIR + q * HEAD, HEAD)

time: 77.7 us -> 71.5 us (0.920)
  Pallas kernels: 73.8 us -> 66.9 us
    pallas_call x1, Pallas kernels: 73.8 us -> 66.9 us  [shards(): pl.pallas_call(kernel, out_shape=(jax.ShapeDtypeStruct((OWN, COLS), BF16)...]
where the time goes in v4:
time: 71.5 us; the launch traced here: 70.6 us
  Pallas kernels  66.9 us (94%)
  local copies, waits for them, and re-layouts  3.15 us (4%)
    pallas_call x1, Pallas kernels, shards(): pl.pallas_call(kernel, out_shape=(jax.ShapeDtypeStruct((OWN, COLS), BF16)...  66.9 us
    unnamed x4, local copies, waits for them, and re-layouts  3.15 us

profile of v4, /device:TPU:1, one launch (start us, length us, event | category | flops | bytes accessed | tf_op | source)
XLA Modules:
  0.0 70.6 jit_solution(3464987480666047079)
XLA Ops:
  0.6 66.9 %muon_back.1 = (bf16[160,2048]{1,0:T(8,128)(2,1)}, bf16[128,5120]{1,0:T(8,128)(2,1)}) custom-call(bf16[128,5120]{1,0:T(8,128)(2,1)} %bitcast.7, bf16[128,5120]{1,0:T(8,128)(2,1)} %cot_h.1, bf16[128,2048]{1,0:T(8,128)(2,1)} %bitcast.11, bf16[5120,2048]{1,0:T(8,128)(2,1)} %bitcast.6, bf16[160,2048]{1,0:T(8,128)(2,1)} %bitcast.9), custom_call_target="tpu_custom_call" | custom-call | tf_op jit(solution)/shard_map/muon_back/pallas_call | solution.py:380
  67.5 0.0 copy-start
  67.5 2.1 %copy.9 = bf16[1,160,2048]{2,1,0:T(8,128)(2,1)} copy(bf16[1,160,2048]{2,1,0:T(8,128)(2,1)} %bitcast.10) | data formatting | bytes 1310720
  69.6 0.0 copy-done
  69.6 1.1 %copy.10 = bf16[1,128,5120]{2,1,0:T(8,128)(2,1)} copy(bf16[1,128,5120]{2,1,0:T(8,128)(2,1)S(1)} %bitcast.8) | data formatting | bytes 2621440
Async XLA Ops:
  67.5 2.1 %copy-start = (bf16[128,5120]{1,0:T(8,128)(2,1)S(1)}, bf16[128,5120]{1,0:T(8,128)(2,1)}, u32[]{:S(2)}) copy-start(bf16[128,5120]{1,0:T(8,128)(2,1)} %get-tuple-element.5) | copy-start | bytes 3932164

commit v5 on v4

--- a/solution.py
+++ b/solution.py
@@ -86,11 +86,11 @@
 
 
 def kernel(
-    acts_h, cot_h, kv_h, w_h, mom_h, upd_o, ig_o,
+    acts_h, cot_h, kv_h, w_h, mom_h, upd_o, gout,
     acts_v, acts_t, acts_g, kv_v, kv_g, w_v, part, trans, acc, rbuf, mom_v, buf,
-    tot, upd, gin, gout, own_v,
+    tot, upd, gin, own_v,
     ld_sem, w_sem, send_sem, kv_recv, kvf_recv, ac_recv, tr_recv, rs_recv,
-    mom_recv, ch_send, ch_recv, ig_sem, t_recv, o_recv,
+    mom_recv, ch_send, ch_recv, t_recv, o_recv,
 ):
     z = lax.axis_index("pipe")
     d = lax.axis_index("dp")
@@ -213,7 +213,6 @@
         def _():
             remote(gout.at[k], gin.at[k], ch_send.at[k], ch_recv.at[k], (z - 1, d)).start()
 
-        pltpu.make_async_copy(gout.at[k], ig_o.at[:, cols(k)], ig_sem.at[k]).start()
 
     done = [0, 0]
 
@@ -362,15 +361,20 @@
     for cp in sends:
         cp.wait_send()
 
-    @pl.loop(0, NCH)
-    def _(k):
-        wait(gout.at[k], ig_sem.at[k])
-
     @pl.when(z > 0)
     def _():
         @pl.loop(0, NCH)
         def _(k):
             remote(gout.at[k], gin.at[k], ch_send.at[k], ch_recv.at[k], (z - 1, d)).wait_send()
+
+
+def store(upd, grads, upd_o, ig_o, sem):
+    copies = [pltpu.make_async_copy(grads.at[k], ig_o.at[:, k * CH:(k + 1) * CH], sem.at[k]) for k in range(NCH)]
+    copies.append(pltpu.make_async_copy(upd, upd_o, sem.at[NCH]))
+    for cp in copies:
+        cp.start()
+    for cp in copies:
+        cp.wait()
 
 
 def shards(acts, cotangent, kv_grads, w_kv, momentum):
@@ -379,25 +383,33 @@
     anyspec = pl.BlockSpec(memory_space=pl.ANY)
     update, grads = pl.pallas_call(
         kernel,
-        out_shape=(jax.ShapeDtypeStruct((OWN, COLS), BF16), jax.ShapeDtypeStruct((TOK, D), BF16)),
+        out_shape=(vmem((OWN, COLS), BF16), vmem((NCH, TOK, CH), BF16)),
         in_specs=[anyspec] * 5,
-        out_specs=(anyspec, anyspec),
+        out_specs=(pl.BlockSpec(memory_space=vmem),) * 2,
         scratch_shapes=[
             vmem((TOK, D), BF16), vmem((D, TOK), BF16), vmem((4 * ROWS, 8 * TOK), BF16),
             vmem((TOK, COLS), BF16), vmem((4, 8 * TOK, PAIR), BF16), vmem((NCH, CH, COLS), BF16),
             vmem((3, 2, 4 * ROWS, HEAD), BF16), vmem((2, 2, 2 * ROWS, HEAD), BF16), vmem((4, 4 * ROWS, PAIR), F32),
             vmem((2, 2, 4 * ROWS, HEAD), BF16), vmem((ROWS, HALF), BF16), vmem((2, 4 * ROWS, HEAD), BF16),
             vmem((2, 4, HEAD, HEAD), F32), vmem((2, 4 * ROWS, HEAD), BF16),
-            vmem((NCH, TOK, CH), BF16), vmem((NCH, TOK, CH), BF16), vmem((NCH, TOK, CH), F32),
+            vmem((NCH, TOK, CH), BF16), vmem((NCH, TOK, CH), F32),
             dma((3,)), dma((NCH,)), dma((96,)), dma((4, 4, 2)), dma((4, 2, 2)), dma((4, 4, 2)),
-            dma((2, 2)), dma((2, 2)), dma((1,)), dma((NCH,)), dma((NCH,)), dma((NCH,)),
+            dma((2, 2)), dma((2, 2)), dma((1,)), dma((NCH,)), dma((NCH,)),
             dma((2, 3)), dma((2, 2, 4)),
         ],
         name="muon_back",
         compiler_params=pltpu.CompilerParams(
-            collective_id=0, has_side_effects=True, vmem_limit_bytes=60 * 1024 * 1024
+            collective_id=0, has_side_effects=True, vmem_limit_bytes=56 * 1024 * 1024
         ),
     )(acts[0], cotangent, kv_grads[0], w_kv[0], momentum[0])
+    update, grads = pl.pallas_call(
+        store,
+        out_shape=(jax.ShapeDtypeStruct((OWN, COLS), BF16), jax.ShapeDtypeStruct((TOK, D), BF16)),
+        in_specs=[pl.BlockSpec(memory_space=vmem)] * 2,
+        out_specs=(anyspec, anyspec),
+        scratch_shapes=[dma((NCH + 1,))],
+        name="store",
+    )(pltpu.with_memory_space_constraint(update, vmem), pltpu.with_memory_space_constraint(grads, vmem))
     return update[None], grads[None]
 
 

time: 71.5 us -> 69.3 us (0.969)
  local copies, waits for them, and re-layouts: 3.15 us -> 0 us
  Pallas kernels: 66.9 us -> 68 us
    unnamed x4 -> x0, local copies, waits for them, and re-layouts: 3.15 us -> none
    pallas_call x1 -> x2, Pallas kernels: 66.9 us -> 68 us  [the longest x1 66.5 us: shards(): pl.pallas_call(kernel, out_shape=(vmem((OWN, COLS), BF16), vmem((NCH, TOK...]
where the time goes in v5:
time: 69.3 us; the launch traced here: 68.6 us
  Pallas kernels  68 us (98%)
    pallas_call x1, Pallas kernels, shards(): pl.pallas_call(kernel, out_shape=(vmem((OWN, COLS), BF16), vmem((NCH, TOK...  66.5 us
    pallas_call x1, Pallas kernels, shards(): pl.pallas_call(store, out_shape=(jax.ShapeDtypeStruct((OWN, COLS), BF16),...  1.45 us

profile of v5, /device:TPU:1, one launch (start us, length us, event | category | flops | bytes accessed | tf_op | source)
XLA Modules:
  0.0 68.6 jit_solution(2274601717970470516)
XLA Ops:
  0.6 66.5 %muon_back.1 = (bf16[160,2048]{1,0:T(8,128)(2,1)S(1)}, bf16[20,128,256]{2,1,0:T(8,128)(2,1)S(1)}) custom-call(bf16[128,5120]{1,0:T(8,128)(2,1)} %bitcast.7, bf16[128,5120]{1,0:T(8,128)(2,1)} %cot_h.1, bf16[128,2048]{1,0:T(8,128)(2,1)} %bitcast.9, bf16[5120,2048]{1,0:T(8,128)(2,1)} %bitcast.6, bf16[160,2048]{1,0:T(8,128)(2,1)} %bitcast.8), custom_call_target="tpu_custom_call" | custom-call | tf_op jit(solution)/shard_map/muon_back/pallas_call | solution.py:384
  67.2 1.4 %store.1 = (bf16[160,2048]{1,0:T(8,128)(2,1)}, bf16[128,5120]{1,0:T(8,128)(2,1)}) custom-call(bf16[160,2048]{1,0:T(8,128)(2,1)S(1)} %get-tuple-element.6.upd, bf16[20,128,256]{2,1,0:T(8,128)(2,1)S(1)} %get-tuple-element.7.grads), custom_call_target="tpu_custom_call" | custom-call | tf_op jit(solution)/shard_map/store/pallas_call | solution.py:405

commit v6 on v5

--- a/solution.py
+++ b/solution.py
@@ -26,18 +26,22 @@
 ORDER = (2, 1, 3, 0)
 PLAN = (
     ((0, 0, 0, 2), (0, 0, 0, 2)),
-    ((5, 5, 4, 6), (0, 0, 1, 5)),
-    ((13, 13, 12, 14), (0, 2, 6, 9)),
-    ((13, 13, 12, 14), (0, 2, 6, 9)),
-    ((17, 17, 16, 18), (0, 4, 8, 12)),
-    ((20, 20, 20, 20), (2, 6, 10, 14)),
-    ((20, 20, 20, 20), (4, 8, 13, 17)),
-    ((20, 20, 20, 20), (5, 10, 15, 19)),
+    ((5, 5, 4, 8), (0, 0, 1, 8)),
+    ((13, 13, 12, 20), (0, 2, 6, 20)),
+    ((13, 13, 12, 20), (0, 2, 6, 20)),
+    ((17, 17, 16, 20), (0, 4, 8, 20)),
+    ((20, 20, 20, 20), (2, 6, 10, 20)),
+    ((20, 20, 20, 20), (4, 8, 13, 20)),
+    ((20, 20, 20, 20), (5, 10, 15, 20)),
     ((20, 20, 20, 20), (8, 13, 18, 20)),
     ((20, 20, 20, 20), (10, 15, 20, 20)),
     ((20, 20, 20, 20), (13, 18, 20, 20)),
     ((20, 20, 20, 20), (13, 19, 20, 20)),
     ((20, 20, 20, 20), (20, 20, 20, 20)),
+    ((20, 20, 20, 20), (5, 10, 15, 20)),
+    ((20, 20, 20, 20), (6, 11, 16, 20)),
+    ((20, 20, 20, 20), (7, 12, 17, 20)),
+    ((20, 20, 20, 20), (8, 13, 17, 20)),
 )
 
 momentum_rate = 0.95
@@ -152,13 +156,11 @@
 
     @pl.loop(0, NCH)
     def _(k):
+        @pl.when(z == 3)
+        def _():
+            pltpu.make_async_copy(cot_h.at[:, cols(k)], gin.at[k], ch_recv.at[k]).start()
+
         pltpu.make_async_copy(w_h.at[pl.ds(pl.multiple_of(k * CH, CH), CH)], w_v.at[k], w_sem.at[k]).start()
-
-    @pl.when(z == 3)
-    def _():
-        @pl.loop(0, NCH)
-        def _(k):
-            pltpu.make_async_copy(cot_h.at[:, cols(k)], gin.at[k], ch_recv.at[k]).start()
 
     pl.semaphore_wait(bar, jnp.where(z > 0, 11, 10))
 
@@ -268,6 +270,18 @@
             part[1, 1, rows, :] = term[:, HEAD:].astype(BF16)
         else:
             acc[o, rows, :] = term
+
+    def transit(q, half):
+        send(part.at[1, q, half_rows(half)], trans.at[q, half], tr_recv.at[q, half], on_r(1 + 2 * half))
+
+    def near_sum(q, way, half):
+        o = 1 + 2 * way
+        rows = half_rows(half)
+        value = acc[o, rows, q * HEAD:(q + 1) * HEAD]
+        if half == way:
+            value = value + trans[q, half].astype(F32)
+        part[o - 1, q, rows, :] = value.astype(BF16)
+        send(part.at[o - 1, q, rows], rbuf.at[q, way, rows], rs_recv.at[q, way, half], on_r(o))
 
     send_acts(0)
     chain(*PLAN[1])
@@ -287,23 +301,25 @@
             for cc in (0, 1):
                 wait(acts_g.at[pl.ds(b * ROWS, ROWS), toks(near(off, cc))], ac_recv.at[b, off, cc])
         block(2, b)
-        if b % 2:
-            half = b // 2
-            for q in range(2):
-                send(part.at[1, q, half_rows(half)], trans.at[q, half], tr_recv.at[q, half], on_r(1 + 2 * half))
         block(1, b)
         block(3, b)
+        if b == 1:
+            for q in range(2):
+                transit(q, 0)
+            near_sum(0, 1, 0)
+        if b == 3:
+            for q in range(2):
+                transit(q, 1)
+            near_sum(1, 1, 0)
+            near_sum(0, 0, 1)
+            near_sum(1, 0, 1)
     pass_kv(0)
     chain(*PLAN[7])
     for q in range(2):
-        head = slice(q * HEAD, (q + 1) * HEAD)
         for half in range(2):
-            o = 1 + 2 * half
             wait(trans.at[q, half], tr_recv.at[q, half])
-            mine, other = half_rows(half), half_rows(1 - half)
-            part[o - 1, q, mine, :] = (acc[o, mine, head] + trans[q, half].astype(F32)).astype(BF16)
-            part[o - 1, q, other, :] = acc[o, other, head].astype(BF16)
-            send(part.at[o - 1, q], rbuf.at[q, half], rs_recv.at[q, half], on_r(o))
+            near_sum(q, half, half)
+            chain(*PLAN[13 + 2 * q + half])
     wait_far(0)
     for b in range(4):
         block(0, b)
@@ -311,8 +327,9 @@
 
     def gram_of(q):
         head = slice(q * HEAD, (q + 1) * HEAD)
-        for half in range(2):
-            wait(rbuf.at[q, half], rs_recv.at[q, half])
+        for way in range(2):
+            for half in range(2):
+                wait(rbuf.at[q, way, half_rows(half)], rs_recv.at[q, way, half])
         total = None
         for b in range(4):
             rows = pl.ds(b * ROWS, ROWS)
@@ -393,8 +410,8 @@
             vmem((2, 2, 4 * ROWS, HEAD), BF16), vmem((ROWS, HALF), BF16), vmem((2, 4 * ROWS, HEAD), BF16),
             vmem((2, 4, HEAD, HEAD), F32), vmem((2, 4 * ROWS, HEAD), BF16),
             vmem((NCH, TOK, CH), BF16), vmem((NCH, TOK, CH), F32),
-            dma((3,)), dma((NCH,)), dma((96,)), dma((4, 4, 2)), dma((4, 2, 2)), dma((4, 4, 2)),
-            dma((2, 2)), dma((2, 2)), dma((1,)), dma((NCH,)), dma((NCH,)),
+            dma((3,)), dma((NCH,)), dma((104,)), dma((4, 4, 2)), dma((4, 2, 2)), dma((4, 4, 2)),
+            dma((2, 2)), dma((2, 2, 2)), dma((1,)), dma((NCH,)), dma((NCH,)),
             dma((2, 3)), dma((2, 2, 4)),
         ],
         name="muon_back",

time: 69.3 us -> 62.1 us (0.90)
  Pallas kernels: 68 us -> 61.3 us
    pallas_call x1, Pallas kernels: 66.5 us -> 59.9 us  [shards(): pl.pallas_call(kernel, out_shape=(vmem((OWN, COLS), BF16), vmem((NCH, TOK...]
where the time goes in v6:
time: 62.1 us; the launch traced here: 62 us
  Pallas kernels  61.3 us (99%)
  between operations  0.64 us (1%)
    pallas_call x1, Pallas kernels, shards(): pl.pallas_call(kernel, out_shape=(vmem((OWN, COLS), BF16), vmem((NCH, TOK...  59.9 us
    pallas_call x1, Pallas kernels, shards(): pl.pallas_call(store, out_shape=(jax.ShapeDtypeStruct((OWN, COLS), BF16),...  1.45 us

profile of v6, /device:TPU:1, one launch (start us, length us, event | category | flops | bytes accessed | tf_op | source)
XLA Modules:
  0.0 62.0 jit_solution(4819773332139820320)
XLA Ops:
  0.6 59.9 %muon_back.1 = (bf16[160,2048]{1,0:T(8,128)(2,1)S(1)}, bf16[20,128,256]{2,1,0:T(8,128)(2,1)S(1)}) custom-call(bf16[128,5120]{1,0:T(8,128)(2,1)} %bitcast.7, bf16[128,5120]{1,0:T(8,128)(2,1)} %cot_h.1, bf16[128,2048]{1,0:T(8,128)(2,1)} %bitcast.9, bf16[5120,2048]{1,0:T(8,128)(2,1)} %bitcast.6, bf16[160,2048]{1,0:T(8,128)(2,1)} %bitcast.8), custom_call_target="tpu_custom_call" | custom-call | tf_op jit(solution)/shard_map/muon_back/pallas_call | solution.py:401
  60.5 1.4 %store.1 = (bf16[160,2048]{1,0:T(8,128)(2,1)}, bf16[128,5120]{1,0:T(8,128)(2,1)}) custom-call(bf16[160,2048]{1,0:T(8,128)(2,1)S(1)} %get-tuple-element.6.upd, bf16[20,128,256]{2,1,0:T(8,128)(2,1)S(1)} %get-tuple-element.7.grads), custom_call_target="tpu_custom_call" | custom-call | tf_op jit(solution)/shard_map/store/pallas_call | solution.py:422

commit v7 on v6

--- a/solution.py
+++ b/solution.py
@@ -27,21 +27,21 @@
 PLAN = (
     ((0, 0, 0, 2), (0, 0, 0, 2)),
     ((5, 5, 4, 8), (0, 0, 1, 8)),
-    ((13, 13, 12, 20), (0, 2, 6, 20)),
-    ((13, 13, 12, 20), (0, 2, 6, 20)),
-    ((17, 17, 16, 20), (0, 4, 8, 20)),
-    ((20, 20, 20, 20), (2, 6, 10, 20)),
-    ((20, 20, 20, 20), (4, 8, 13, 20)),
-    ((20, 20, 20, 20), (5, 10, 15, 20)),
+    ((13, 13, 12, 20), (0, 3, 7, 20)),
+    ((13, 13, 12, 20), (0, 3, 7, 20)),
+    ((17, 17, 16, 20), (0, 5, 9, 20)),
+    ((20, 20, 20, 20), (2, 7, 11, 20)),
+    ((20, 20, 20, 20), (4, 9, 13, 20)),
+    ((20, 20, 20, 20), (5, 11, 15, 20)),
+    ((20, 20, 20, 20), (8, 14, 20, 20)),
+    ((20, 20, 20, 20), (11, 17, 20, 20)),
+    ((20, 20, 20, 20), (13, 20, 20, 20)),
+    ((20, 20, 20, 20), (13, 20, 20, 20)),
+    ((20, 20, 20, 20), (20, 20, 20, 20)),
+    ((20, 20, 20, 20), (5, 11, 15, 20)),
+    ((20, 20, 20, 20), (6, 12, 16, 20)),
+    ((20, 20, 20, 20), (7, 12, 17, 20)),
     ((20, 20, 20, 20), (8, 13, 18, 20)),
-    ((20, 20, 20, 20), (10, 15, 20, 20)),
-    ((20, 20, 20, 20), (13, 18, 20, 20)),
-    ((20, 20, 20, 20), (13, 19, 20, 20)),
-    ((20, 20, 20, 20), (20, 20, 20, 20)),
-    ((20, 20, 20, 20), (5, 10, 15, 20)),
-    ((20, 20, 20, 20), (6, 11, 16, 20)),
-    ((20, 20, 20, 20), (7, 12, 17, 20)),
-    ((20, 20, 20, 20), (8, 13, 17, 20)),
 )
 
 momentum_rate = 0.95
@@ -301,15 +301,14 @@
             for cc in (0, 1):
                 wait(acts_g.at[pl.ds(b * ROWS, ROWS), toks(near(off, cc))], ac_recv.at[b, off, cc])
         block(2, b)
+        if b % 2:
+            for q in range(2):
+                transit(q, b // 2)
         block(1, b)
         block(3, b)
         if b == 1:
-            for q in range(2):
-                transit(q, 0)
             near_sum(0, 1, 0)
         if b == 3:
-            for q in range(2):
-                transit(q, 1)
             near_sum(1, 1, 0)
             near_sum(0, 0, 1)
             near_sum(1, 0, 1)
@@ -347,12 +346,13 @@
             wait(tot.at[q, mod4(pg + 4 - o)], t_recv.at[q, o - 1])
         scale = 0.2 * math.sqrt(max(D, HEAD))
         high, mid, low = split(newton_schulz((tot[q, 0] + tot[q, 1]) + (tot[q, 2] + tot[q, 3]), scale))
+        wide = jnp.concatenate([high, mid], 0)
         place = pl.ds(pl.multiple_of(mycol + pr * PAIR + q * HEAD, HEAD), HEAD)
         for o in ORDER:
             first = pl.multiple_of(mod4(pr + o) * ROWS, ROWS)
             value = buf[q, pl.ds(first, ROWS), :]
-            total = jnp.dot(value, low, preferred_element_type=F32) + jnp.dot(value, mid, preferred_element_type=F32)
-            upd[q, pl.ds(first, ROWS), :] = (total + jnp.dot(value, high, preferred_element_type=F32)).astype(BF16)
+            total = jnp.dot(jnp.concatenate([value, value], 1), wide, preferred_element_type=F32)
+            upd[q, pl.ds(first, ROWS), :] = (total + jnp.dot(value, low, preferred_element_type=F32)).astype(BF16)
             same = upd.at[q, pl.ds(pl.multiple_of(first + myrow, OWN), OWN)]
             cross = upd.at[q, pl.ds(pl.multiple_of(first + sibrow, OWN), OWN)]
             if o:

time: 62.1 us -> 60.7 us (0.977)
  Pallas kernels: 61.3 us -> 60 us
    pallas_call x1, Pallas kernels: 59.9 us -> 58.5 us  [shards(): pl.pallas_call(kernel, out_shape=(vmem((OWN, COLS), BF16), vmem((NCH, TOK...]
where the time goes in v7:
time: 60.7 us; the launch traced here: 60.6 us
  Pallas kernels  60 us (99%)
  between operations  0.64 us (1%)
    pallas_call x1, Pallas kernels, shards(): pl.pallas_call(kernel, out_shape=(vmem((OWN, COLS), BF16), vmem((NCH, TOK...  58.5 us
    pallas_call x1, Pallas kernels, shards(): pl.pallas_call(store, out_shape=(jax.ShapeDtypeStruct((OWN, COLS), BF16),...  1.45 us

profile of v7, /device:TPU:1, one launch (start us, length us, event | category | flops | bytes accessed | tf_op | source)
XLA Modules:
  0.0 60.6 jit_solution(16435339276191247392)
XLA Ops:
  0.6 58.5 %muon_back.1 = (bf16[160,2048]{1,0:T(8,128)(2,1)S(1)}, bf16[20,128,256]{2,1,0:T(8,128)(2,1)S(1)}) custom-call(bf16[128,5120]{1,0:T(8,128)(2,1)} %bitcast.7, bf16[128,5120]{1,0:T(8,128)(2,1)} %cot_h.1, bf16[128,2048]{1,0:T(8,128)(2,1)} %bitcast.9, bf16[5120,2048]{1,0:T(8,128)(2,1)} %bitcast.6, bf16[160,2048]{1,0:T(8,128)(2,1)} %bitcast.8), custom_call_target="tpu_custom_call" | custom-call | tf_op jit(solution)/shard_map/muon_back/pallas_call | solution.py:401
  59.2 1.4 %store.1 = (bf16[160,2048]{1,0:T(8,128)(2,1)}, bf16[128,5120]{1,0:T(8,128)(2,1)}) custom-call(bf16[160,2048]{1,0:T(8,128)(2,1)S(1)} %get-tuple-element.6.upd, bf16[20,128,256]{2,1,0:T(8,128)(2,1)S(1)} %get-tuple-element.7.grads), custom_call_target="tpu_custom_call" | custom-call | tf_op jit(solution)/shard_map/store/pallas_call | solution.py:422

commit v8 on v7

--- a/solution.py
+++ b/solution.py
@@ -365,8 +365,8 @@
     gram_of(0)
     chain(*PLAN[9])
     gram_of(1)
+    chain(*PLAN[10])
     iterate(0)
-    chain(*PLAN[10])
     iterate(1)
     chain(*PLAN[12])
     for q in range(2):

time: 60.7 us -> 60.7 us (level)
  no operation moved by 1% of the time
where the time goes in v8:
time: 60.7 us; the launch traced here: 60.6 us
  Pallas kernels  59.9 us (99%)
  between operations  0.64 us (1%)
    pallas_call x1, Pallas kernels, shards(): pl.pallas_call(kernel, out_shape=(vmem((OWN, COLS), BF16), vmem((NCH, TOK...  58.5 us
    pallas_call x1, Pallas kernels, shards(): pl.pallas_call(store, out_shape=(jax.ShapeDtypeStruct((OWN, COLS), BF16),...  1.45 us

profile of v8, /device:TPU:1, one launch (start us, length us, event | category | flops | bytes accessed | tf_op | source)
XLA Modules:
  0.0 60.6 jit_solution(17448401450512795603)
XLA Ops:
  0.6 58.5 %muon_back.1 = (bf16[160,2048]{1,0:T(8,128)(2,1)S(1)}, bf16[20,128,256]{2,1,0:T(8,128)(2,1)S(1)}) custom-call(bf16[128,5120]{1,0:T(8,128)(2,1)} %bitcast.7, bf16[128,5120]{1,0:T(8,128)(2,1)} %cot_h.1, bf16[128,2048]{1,0:T(8,128)(2,1)} %bitcast.9, bf16[5120,2048]{1,0:T(8,128)(2,1)} %bitcast.6, bf16[160,2048]{1,0:T(8,128)(2,1)} %bitcast.8), custom_call_target="tpu_custom_call" | custom-call | tf_op jit(solution)/shard_map/muon_back/pallas_call | solution.py:401
  59.1 1.4 %store.1 = (bf16[160,2048]{1,0:T(8,128)(2,1)}, bf16[128,5120]{1,0:T(8,128)(2,1)}) custom-call(bf16[160,2048]{1,0:T(8,128)(2,1)S(1)} %get-tuple-element.6.upd, bf16[20,128,256]{2,1,0:T(8,128)(2,1)S(1)} %get-tuple-element.7.grads), custom_call_target="tpu_custom_call" | custom-call | tf_op jit(solution)/shard_map/store/pallas_call | solution.py:422
